TPU v7x, 128 devices: a whole 4x4x4 slice. The times are simulated.
128 devices in a mesh: seq: 16 (over z, y_hi, core), grp: 8 (over x, y_lo).
Axes of the slice: x: 4, y: 4 (y_hi: 2, y_lo: 2; y = y_hi * 2 + y_lo), z: 4, core: 2. Of those that a mesh axis runs over, the one named last changes fastest.
Arguments:
- tokens: bfloat16 [262144, 1280], P(('seq', 'grp')), may hold values from -27 to 27
- slot_keys: bfloat16 [1280, 512], replicated, may hold values from -1.5 to 1.5
- norm_gain: float32 [128, 1280], P(('seq', 'grp')), may hold values from 0.1 to 1.9
- w_in: bfloat16 [128, 1280, 2560], P(('seq', 'grp')), may hold values from -0.15625 to 0.15625
- w_out: bfloat16 [128, 2560, 1280], P(('seq', 'grp')), may hold values from -0.125 to 0.125
Outputs:
- mixed: bfloat16 [262144, 1280], P(('seq', 'grp'))
All inputs are finite; a program needn't handle non-finite values.
Results may differ from a plain program's by a relative error of at most 0.007.
Values may be sent and summed in bfloat16 or wider, within the bound.
A program may use at most 128 MiB of HBM per device.

v0:
```python
import jax
import jax.numpy as jnp
from jax import lax
from jax.sharding import PartitionSpec as P


def in_one_piece(arrays, axis, split_dim, concat_dim, along):
    columns = [a.reshape(*a.shape[:along], -1) for a in arrays]
    both = jnp.concatenate(columns, axis=along)
    out, at, finished = (
        lax.all_to_all(both, axis, split_axis=split_dim, concat_axis=concat_dim, tiled=True),
        0,
        [],
    )
    for a, column in zip(arrays, columns):
        piece = out[..., at : at + column.shape[along]]
        finished.append(piece.reshape(*piece.shape[:along], *a.shape[along:]))
        at += column.shape[along]
    return tuple(finished)


def on_device(tokens, slot_keys, norm_gain, w_in, w_out):
    devices = lax.axis_size(("seq", "grp"))
    logits = jnp.dot(tokens, slot_keys, preferred_element_type=jnp.float32)
    per_dev = logits.shape[1] // devices
    maxima = jnp.max(logits, axis=0)
    scores = jnp.exp(logits - maxima[None, :])
    totals = jnp.sum(scores, axis=0)
    weights = scores.astype(jnp.bfloat16)
    dims = (((0,), (0,)), ((), ()))
    numer_local = lax.dot_general(weights, tokens, dims, preferred_element_type=jnp.float32)
    parts, peaks, sums = in_one_piece((numer_local, maxima, totals), ("seq", "grp"), 0, 0, 1)
    peaks = peaks.reshape(devices, per_dev)
    factor = jnp.exp(peaks - jnp.max(peaks, axis=0, keepdims=True))
    numer = jnp.sum(parts.reshape(devices, per_dev, -1) * factor[:, :, None], axis=0)
    own_total = jnp.sum(sums.reshape(devices, per_dev) * factor, axis=0)
    slot_in = numer / own_total[:, None]
    normed = (slot_in * norm_gain[0][None, :]).astype(jnp.bfloat16)
    hidden = jax.nn.gelu(jnp.dot(normed, w_in[0], preferred_element_type=jnp.float32)).astype(
        jnp.bfloat16
    )
    expert_out = jnp.dot(hidden, w_out[0], preferred_element_type=jnp.float32).astype(jnp.bfloat16)
    row_top = jnp.max(logits, axis=1, keepdims=True)
    row_exp = jnp.exp(logits - row_top)
    combine = (row_exp / jnp.sum(row_exp, axis=1, keepdims=True)).astype(jnp.bfloat16)
    gathered = lax.all_gather(expert_out, ("seq", "grp"), axis=0, tiled=True)
    mixed = jnp.dot(combine, gathered, preferred_element_type=jnp.float32)
    return mixed.astype(jnp.bfloat16)


def solution(mesh):
    return jax.shard_map(
        on_device,
        mesh=mesh,
        in_specs=(
            P(("seq", "grp"), None),
            P(),
            P(("seq", "grp"), None),
            P(("seq", "grp"), None, None),
            P(("seq", "grp"), None, None),
        ),
        out_specs=P(("seq", "grp"), None),
        check_vma=False,
    )
```

profile of v0, /device:TPU:1, one launch (start us, length us, event | category | flops | bytes accessed | tf_op | source)
XLA Modules:
  0.0 423.7 jit_solution(511834206281356095)
XLA Ops:
  6.5 0.0 copy-start
  6.5 1.3 copy-done
  7.9 7.1 %fusion.44 = (f32[2048]{0:T(1024)S(1)}, f32[512]{0:T(512)S(1)}, f32[2048,512]{1,0:T(8,128)}) fusion(bf16[2048,1280]{1,0:T(8,128)(2,1)} %param.5, bf16[1280,512]{1,0:T(8,128)(2,1)S(1)} %copy-done), kind=kOutput, calls=%fused_computation.42 | convolution fusion | flops 2686449152 | bytes 10758144 | tf_op jit(solution)/shard_map/dot_general | solution.py:24
  14.9 0.3 concatenate.14
  15.3 0.0 copy-start.1
  15.3 8.4 %fusion.13 = f32[512,1280]{1,0:T(8,128)} fusion(bf16[2048,1280]{1,0:T(8,128)(2,1)} %param.5, f32[2048,512]{1,0:T(8,128)} %get-tuple-element.13, f32[512]{0:T(512)S(1)} %get-tuple-element.8), kind=kOutput, calls=%fused_computation.14 | convolution fusion | flops 2686451712 | bytes 12060672 | tf_op jit(solution)/shard_map/dot_general | solution.py:31
  23.6 0.0 copy-done.1
  23.6 1.6 fusion.4
  25.2 0.3 concatenate.15
  25.6 3.9 concatenate.10
  29.5 5.6 %concatenate.13 = f32[128,4,1282]{2,1,0:T(4,128)} concatenate(f32[128,4,1280]{2,1,0:T(4,128)} %concatenate.10, f32[128,4,1]{2,1,0:T(4,128)S(1)} %concatenate.14, f32[128,4,1]{2,1,0:T(4,128)S(1)} %concatenate.15), dimensions={2} | concatenate | bytes 5251072 | tf_op jit(solution)/shard_map/concatenate | solution.py:9
  35.1 0.0 copy-start.2
  35.1 11.9 %all-to-all-start = ((f32[128,4,1282]{2,1,0:T(4,128)}), f32[128,4,1282]{2,1,0:T(4,128)}, u32[]{:S(2)}, u32[]{:S(2)}) async-start(f32[128,4,1282]{2,1,0:T(4,128)} %concatenate.13), calls=%async_computation | async-start | bytes 5767168 | tf_op jit(solution)/shard_map/all_to_all | solution.py:11
  47.0 0.2 all-gather.3.cloned.1.call-start
  47.2 0.0 copy-done.2
  47.3 37.5 %all-to-all-done = f32[128,4,1282]{2,1,0:T(4,128)} async-done(((f32[128,4,1282]{2,1,0:T(4,128)}), f32[128,4,1282]{2,1,0:T(4,128)}, u32[]{:S(2)}, u32[]{:S(2)}) %all-to-all-start) | async-done | bytes 2625568 | tf_op jit(solution)/shard_map/all_to_all | solution.py:11
  84.8 4.4 %all_to_all.7 = f32[512,1282]{1,0:T(8,128)} reshape(f32[128,4,1282]{2,1,0:T(4,128)} %all-to-all-done) | data formatting | bytes 5251072 | tf_op jit(solution)/shard_map/all_to_all | solution.py:11
  89.2 1.3 slice_reduce_fusion
  90.5 3.4 slice.12
  93.9 3.9 reshape.37
  97.8 0.1 reshape_reshape.7
  97.9 0.1 reshape_reshape.6
  98.1 2.3 multiply_reduce_fusion
  100.5 7.3 %fusion.10 = bf16[1,4,1280]{2,1,0:T(4,128)(2,1)} fusion(bf16[1,2560,1280]{2,1,0:T(8,128)(2,1)} %param.9, bf16[1,1280,2560]{2,1,0:T(8,128)(2,1)} %param.8, f32[4,1280]{1,0:T(4,128)S(1)} %multiply_reduce_fusion, f32[1280]{0:T(1024)S(1)} %reduce.2, f32[4]{0:T(128)S(1)} %get-tuple-element.11), kind=kOutput, calls=%fused_computation.13 | convolution fusion | flops 52541440 | bytes 13143056 | tf_op jit(solution)/shard_map/dot_general | solution.py:42
  107.8 0.0 all-gather.3.cloned.1.call-update
  107.8 298.9 %all-gather.3.cloned.1.call-done = bf16[128,4,1280]{2,1,0:T(4,128)(2,1)} async-done(((bf16[1,4,1280]{2,1,0:T(4,128)(2,1)}), bf16[128,4,1280]{2,1,0:T(4,128)(2,1)}) %all-gather.3.cloned.1.call-update) | async-done | bytes 1310736 | tf_op jit(solution)/shard_map/all_gather | solution.py:46
  406.7 2.5 reshape.39
  409.2 7.7 %convolution_convert_fusion = bf16[2048,1280]{1,0:T(8,128)(2,1)} fusion(bf16[512,1280]{1,0:T(8,128)(2,1)S(1)} %reshape.39, f32[2048,512]{1,0:T(8,128)} %get-tuple-element.13, f32[2048]{0:T(1024)S(1)} %get-tuple-element.5, f32[2048]{0:T(1024)S(1)} %get-tuple-element.7), kind=kOutput, calls=%fused_computation | convolution fusion | flops 2690121728 | bytes 10764288 | tf_op jit(solution)/shard_map/dot_general | solution.py:47
  (3 shorter events, 0.1 us)
Async XLA Ops:
  6.5 1.3 copy-start
  15.3 8.4 %copy-start.1 = (f32[2048,512]{1,0:T(8,128)S(1)}, f32[2048,512]{1,0:T(8,128)}, u32[]{:S(2)}) copy-start(f32[2048,512]{1,0:T(8,128)} %get-tuple-element.13) | copy-start | bytes 12582916
  35.1 12.1 %copy-start.2 = (f32[1,1280]{1,0:T(1,128)S(1)}, f32[1,1280]{1,0:T(1,128)}, u32[]{:S(2)}) copy-start(f32[1,1280]{1,0:T(1,128)} %param.7) | copy-start | bytes 15364
  35.1 49.7 %all-to-all-start = ((f32[128,4,1282]{2,1,0:T(4,128)}), f32[128,4,1282]{2,1,0:T(4,128)}, u32[]{:S(2)}, u32[]{:S(2)}) async-start(f32[128,4,1282]{2,1,0:T(4,128)} %concatenate.13), calls=%async_computation | async-start | bytes 5767168 | tf_op jit(solution)/shard_map/all_to_all | solution.py:11
  47.0 359.7 %all-gather.3.cloned.1.call-start = ((), (), s32[]{:S(2)}) async-start(), calls=%async_computation.1 | async-start | bytes 1320960 | tf_op jit(solution)/shard_map/all_gather | solution.py:46
Sparse Core Ops, SparseCore 0:
  107.9 298.7 all-gather.2
where the time goes:
time: 424 us
  waiting for transfers between devices  336 us (79%)
  matrix products  30.5 us (7%)
  local copies, waits for them, and re-layouts  27.3 us (6%)
  between operations  13.5 us (3%)
  starting transfers between devices  12.1 us (3%)
    all_gather x1, waiting for transfers between devices, on_device(): gathered = lax.all_gather(expert_out, ('seq', 'grp'), axis=0, tiled=True)  299 us
    all_to_all x1, waiting for transfers between devices, in_one_piece(): lax.all_to_all(both, axis, split_axis=split_dim, concat_axis=concat_dim,...  37.5 us
    all_to_all x1, starting transfers between devices, in_one_piece(): lax.all_to_all(both, axis, split_axis=split_dim, concat_axis=concat_dim,...  11.9 us
    concatenate x4, local copies, waits for them, and re-layouts, in_one_piece(): both = jnp.concatenate(columns, axis=along)  10.2 us
  transfers between devices with their start and end apart: 2, of which 2 were waited for; matrix products, arithmetic and copies ran while one was open for 0% of the time, Pallas kernels for 0%

commit v1 on v0

v1 whole, which is shorter than its diff:
```python
import jax
import jax.numpy as jnp
from jax import lax
from jax.experimental import pallas as pl
from jax.experimental.pallas import tpu as pltpu
from jax.sharding import PartitionSpec as P

F32 = jnp.float32
BF16 = jnp.bfloat16
MESH = pl.DeviceIdType.MESH
TOK, D, FF, SLOTS = 2048, 1280, 2560, 512
TILE = 256
TILES = TOK // TILE
WIDE = 256
CHUNKS = D // WIDE
SPLIT = 512
ORDER = (2, 0, 3, 1, 4)
S_AUX0, S_AUXA, S_AUXB, S_AUXY = 0, 1, 7, 13
S_CORE = 16
S_ONE = 21
S_TWO = 36
S_Y = 42
S_GY = 45
S_G2 = 48
S_G3 = 54
S_GC = 60
N_SEM = 68


def place():
    seq = lax.axis_index("seq")
    grp = lax.axis_index("grp")
    return {"z": seq // 4, "yh": (seq // 2) % 2, "c": seq % 2, "x": grp // 2, "yl": grp % 2}


def device(at):
    return ((at["z"] * 2 + at["yh"]) * 2 + at["c"], at["x"] * 2 + at["yl"])


def ring(me, axis, d):
    at = dict(me)
    if axis == "y":
        to = (me["yh"] * 2 + me["yl"] + d) % 4
        at["yh"], at["yl"] = to // 2, to % 2
    else:
        to = (me[axis] + d) % 4
        at[axis] = to
    return device(at), to


def kernel(tok_h, key_h, gain, win_h, wout_h, g_out, comb_out,
           tok, key, logit, sct, comb, numer, win, wout, aux, auxr, fcol,
           csend, crecv, s1, r1, s2x, s2z, r2x, r2z, ysend, yrecv, gy, g,
           load_sem, comb_sem, send_sem, recv_sem):
    me = place()
    my = me["yh"] * 2 + me["yl"]
    other = dict(me)
    other["c"] = 1 - me["c"]
    partner = device(other)

    key_in = pltpu.make_async_copy(key_h, key, load_sem.at[0])
    key_in.start()
    tok_in = []
    for t in range(TILES):
        rows = pl.ds(t * TILE, TILE)
        tok_in.append(pltpu.make_async_copy(tok_h.at[rows], tok.at[rows], load_sem.at[1 + t]))
        tok_in[-1].start()
    win_in = pltpu.make_async_copy(win_h.at[0], win, load_sem.at[TILES + 1])
    wout_in = pltpu.make_async_copy(wout_h.at[0], wout, load_sem.at[TILES + 2])

    barrier = pltpu.get_barrier_semaphore()
    pl.semaphore_signal(barrier, inc=1, device_id=partner, device_id_type=MESH)
    for axis in "xzy":
        for d in (1, 2, 3):
            pl.semaphore_signal(barrier, inc=1, device_id=ring(me, axis, d)[0], device_id_type=MESH)

    def remote(src, dst, sem, target):
        return pltpu.make_async_remote_copy(
            src_ref=src, dst_ref=dst, send_sem=send_sem.at[sem], recv_sem=recv_sem.at[sem],
            device_id=target, device_id_type=MESH)

    started = []

    def send(src, dst, sem, target):
        copy = remote(src, dst, sem, target)
        copy.start()
        started.append(copy)
        return copy

    key_in.wait()
    peak8 = jnp.full((8, SLOTS), -jnp.inf, F32)
    for t in range(TILES):
        rows = pl.ds(t * TILE, TILE)
        tok_in[t].wait()
        part = jnp.dot(tok[rows], key[...], preferred_element_type=F32)
        logit[rows] = part
        peak8 = jnp.maximum(peak8, jnp.max(part.reshape(TILE // 8, 8, SLOTS), axis=0))
    win_in.start()
    wout_in.start()
    peak = jnp.max(peak8, axis=0, keepdims=True)

    def score_step(t, total8):
        rows = pl.ds(pl.multiple_of(t * TILE, TILE), TILE)
        scores = jnp.exp(logit[rows] - peak)
        sct[:, rows] = scores.T.astype(BF16)
        return total8 + jnp.sum(scores.reshape(TILE // 8, 8, SLOTS), axis=0)

    total8 = lax.fori_loop(0, TILES, score_step, jnp.zeros((8, SLOTS), F32))
    total = jnp.sum(total8, axis=0, keepdims=True)

    row = lax.broadcasted_iota(jnp.int32, (8, SLOTS), 0)

    def put_aux(slot, top, tot):
        aux[slot] = jnp.where(row == 0, top, jnp.where(row == 1, tot, 0.0))

    put_aux(0, peak, total)
    pl.semaphore_wait(barrier, 10)
    send(aux.at[0], auxr.at[0], S_AUX0, partner)

    def merge_aux(own, others, col):
        tops = [own[0:1]] + [o[0:1] for o in others]
        tots = [own[1:2]] + [o[1:2] for o in others]
        top = tops[0]
        for p in tops[1:]:
            top = jnp.maximum(top, p)
        factors = [jnp.exp(p - top) for p in tops]
        tot = factors[0] * tots[0]
        for f, t in zip(factors[1:], tots[1:]):
            tot = tot + f * t
        line = lax.broadcasted_iota(jnp.int32, (128, SLOTS), 0)
        block = jnp.zeros((128, SLOTS), F32)
        for i, f in enumerate(factors):
            block = jnp.where(line == i, f, block)
        fcol[col] = block.T.reshape(4, 2, 2, 4, 8, 128)
        return top, tot

    core_copies, one_copies = {}, {}

    def core_send(k):
        core_copies[k] = send(csend.at[k], crecv.at[k], S_CORE + k, partner)

    def numer_chunk(k, slot):
        cols = pl.ds(k * WIDE, WIDE)
        part = jnp.dot(sct[...], tok[:, cols], preferred_element_type=F32)
        numer[slot] = part.reshape(4, 2, 2, 4, 8, WIDE)
        csend[k] = numer[slot, :, :, 1 - me["c"]].astype(BF16)
        core_send(k)

    def core_merge(k, slot):
        core_copies[k].wait_recv()
        f = fcol[0, :, :, me["c"]]
        both = (numer[slot, :, :, me["c"]] * f[..., 0:1]
                + crecv[k].astype(F32) * f[..., 1:2]).astype(BF16)
        first = k * WIDE < SPLIT
        for i in range(4):
            if first:
                s1[k, i] = both[:, :, i].reshape(8, 8, WIDE)
            else:
                s1[k, i] = both[i].reshape(8, 8, WIDE)
        one_copies[k] = []
        for d in (1, 2, 3):
            target, to = ring(me, "x" if first else "z", d)
            one_copies[k].append(send(s1.at[k, to], r1.at[k, d - 1], S_ONE + 3 * k + d - 1, target))

    aux_one = []
    for i, k in enumerate(ORDER):
        numer_chunk(k, i % 2)
        if i == 0:
            remote(aux.at[0], auxr.at[0], S_AUX0, partner).wait_recv()
            top, tot = merge_aux(aux[0], [auxr[0]], 0)
            put_aux(1, top, tot)
            for j, axis in enumerate("xz"):
                for d in (1, 2, 3):
                    n = 3 * j + d - 1
                    aux_one.append(send(aux.at[1], auxr.at[1 + n], S_AUXA + n, ring(me, axis, d)[0]))
        else:
            core_merge(ORDER[i - 1], (i - 1) % 2)
    core_merge(ORDER[-1], (CHUNKS - 1) % 2)

    for copy in aux_one:
        copy.wait_recv()
    aux_two = []
    for j, axis in enumerate("zx"):
        top, tot = merge_aux(aux[1], [auxr[1 + 3 * j + n] for n in range(3)], 1 + j)
        put_aux(2 + j, top, tot)
        for d in (1, 2, 3):
            n = 3 * j + d - 1
            aux_two.append(send(aux.at[2 + j], auxr.at[7 + n], S_AUXB + n, ring(me, axis, d)[0]))


    def combine_step(t, carry):
        rows = pl.ds(pl.multiple_of(t * TILE, TILE), TILE)
        block = logit[rows]
        e = jnp.exp(block - jnp.max(block, axis=1, keepdims=True))
        comb[rows] = (e / jnp.sum(e, axis=1, keepdims=True)).astype(BF16)
        return carry

    lax.fori_loop(0, TILES, combine_step, 0)
    comb_copy = pltpu.make_async_copy(comb, comb_out, comb_sem.at[0])
    comb_copy.start()

    for copy in aux_two:
        copy.wait_recv()
    for j in range(2):
        top, tot = merge_aux(aux[2 + j], [auxr[7 + 3 * j + n] for n in range(3)], 3 + j)
        if j == 0:
            put_aux(4, top, tot)
    aux_y = [send(aux.at[4], auxr.at[13 + d - 1], S_AUXY + d - 1, ring(me, "y", d)[0]) for d in (1, 2, 3)]

    def stage_one(k):
        first = k * WIDE < SPLIT
        for copy in one_copies[k]:
            copy.wait_recv()
        if first:
            f = fcol[1, :, :, me["c"], me["x"]].reshape(8, 8, 128)
            out = s1[k, me["x"]].astype(F32) * f[..., 0:1]
        else:
            f = fcol[2, me["z"], :, me["c"]].reshape(8, 8, 128)
            out = s1[k, me["z"]].astype(F32) * f[..., 0:1]
        for d in (1, 2, 3):
            out = out + r1[k, d - 1].astype(F32) * f[..., d : d + 1]
        out = out.astype(BF16).reshape((4, 2, 8, WIDE) if first else (2, 4, 8, WIDE))
        at = k * WIDE if first else k * WIDE - SPLIT
        for i in range(4):
            if first:
                s2x[i, :, :, at : at + WIDE] = out[i]
            else:
                s2z[i, :, :, at : at + WIDE] = out[:, i]

    two = []
    for k in (2, 3, 4):
        stage_one(k)
    for d in (1, 2, 3):
        target, to = ring(me, "x", d)
        two.append(send(s2z.at[to], r2z.at[d - 1], S_TWO + 3 + d - 1, target))
    for k in (0, 1):
        stage_one(k)
    for d in (1, 2, 3):
        target, to = ring(me, "z", d)
        two.append(send(s2x.at[to], r2x.at[d - 1], S_TWO + d - 1, target))
    for copy in aux_y:
        copy.wait_recv()
    top, tot = merge_aux(aux[4], [auxr[13 + n] for n in range(3)], 5)
    line = lax.broadcasted_iota(jnp.int32, (128, SLOTS), 0)
    fcol[6] = jnp.where(line == 0, tot, 0.0).T.reshape(4, 2, 2, 4, 8, 128)

    for copy in two:
        copy.wait_recv()
    fx = fcol[3, me["z"], :, me["c"], me["x"]]
    fz = fcol[4, me["z"], :, me["c"], me["x"]]
    outx = s2x[me["z"]].astype(F32) * fx[..., 0:1]
    outz = s2z[me["x"]].astype(F32) * fz[..., 0:1]
    for d in (1, 2, 3):
        outx = outx + r2x[d - 1].astype(F32) * fx[..., d : d + 1]
        outz = outz + r2z[d - 1].astype(F32) * fz[..., d : d + 1]
    ysend[:, :, 0:SPLIT] = outx.astype(BF16)
    ysend[:, :, SPLIT:D] = outz.astype(BF16)

    last = []
    for d in (1, 2, 3):
        target, to = ring(me, "y", d)
        last.append(send(ysend.at[to // 2], yrecv.at[d - 1], S_Y + d - 1, target))
    fy = fcol[5, me["z"], me["yh"], me["c"], me["x"]]
    own_total = fcol[6, me["z"], me["yh"], me["c"], me["x"]]
    slot_in = ysend[me["yh"]].astype(F32) * fy[:, 0:1]
    for copy in last:
        copy.wait_recv()
    for d in (1, 2, 3):
        slot_in = slot_in + yrecv[d - 1].astype(F32) * fy[:, d : d + 1]
    slot_in = slot_in / own_total[:, 0:1]

    normed = (slot_in * gain[...]).astype(BF16)
    win_in.wait()
    wout_in.wait()
    hidden = jax.nn.gelu(jnp.dot(normed, win[...], preferred_element_type=F32)).astype(BF16)
    out = jnp.dot(hidden, wout[...], preferred_element_type=F32)
    half = lax.broadcasted_iota(jnp.int32, (8, D), 0) // 4
    gy[my] = jnp.where(half == me["yl"], out, 0.0).astype(BF16)

    back = []
    for d in (1, 2, 3):
        back.append(send(gy.at[my], gy.at[my], S_GY + d - 1, ring(me, "y", d)[0]))
    for copy in back:
        copy.wait_recv()
    for i in range(2):
        g[me["z"], i, me["c"], me["x"]] = gy[2 * i] + gy[2 * i + 1]
    left, right = pl.ds(0, SPLIT), pl.ds(SPLIT, D - SPLIT)
    g2 = []
    for d in (1, 2, 3):
        mine = g.at[me["z"], :, me["c"], me["x"], :, right]
        g2.append(send(mine, mine, S_G2 + 3 + d - 1, ring(me, "x", d)[0]))
    for d in (1, 2, 3):
        mine = g.at[me["z"], :, me["c"], me["x"], :, left]
        g2.append(send(mine, mine, S_G2 + d - 1, ring(me, "z", d)[0]))
    for copy in g2[0:3]:
        copy.wait_recv()
    g3 = []
    for d in (1, 2, 3):
        mine = g.at[me["z"], :, me["c"], :, :, right]
        g3.append(send(mine, mine, S_G3 + 3 + d - 1, ring(me, "z", d)[0]))
    for copy in g2[3:6]:
        copy.wait_recv()
    for d in (1, 2, 3):
        mine = g.at[:, :, me["c"], me["x"], :, left]
        g3.append(send(mine, mine, S_G3 + d - 1, ring(me, "x", d)[0]))
    gc = []

    def pass_on(d):
        z = (me["z"] + 4 - d) % 4
        x = (me["x"] + 4 - d) % 4
        a = g.at[z, :, me["c"], :, :, right]
        b = g.at[:, :, me["c"], x, :, left]
        gc.append(send(a, a, S_GC + d, partner))
        gc.append(send(b, b, S_GC + 4 + d, partner))

    pass_on(0)
    for d in (1, 2, 3):
        g3[d - 1].wait_recv()
        g3[3 + d - 1].wait_recv()
        pass_on(d)
    for copy in gc:
        copy.wait_recv()
    g_copy = pltpu.make_async_copy(g, g_out, comb_sem.at[1])
    g_copy.start()
    for copy in started:
        copy.wait_send()
    comb_copy.wait()
    g_copy.wait()


def on_device(tokens, slot_keys, norm_gain, w_in, w_out):
    anywhere = pl.BlockSpec(memory_space=pl.ANY)
    vmem = pltpu.VMEM
    gathered, combine = pl.pallas_call(
        kernel,
        out_shape=(
            jax.ShapeDtypeStruct((4, 2, 2, 4, 8, D), BF16),
            jax.ShapeDtypeStruct((TOK, SLOTS), BF16),
        ),
        in_specs=[anywhere, anywhere, pl.BlockSpec(memory_space=vmem), anywhere, anywhere],
        out_specs=(anywhere, anywhere),
        scratch_shapes=[
            vmem((TOK, D), BF16),
            vmem((D, SLOTS), BF16),
            vmem((TOK, SLOTS), F32),
            vmem((SLOTS, TOK), BF16),
            vmem((TOK, SLOTS), BF16),
            vmem((2, 4, 2, 2, 4, 8, WIDE), F32),
            vmem((D, FF), BF16),
            vmem((FF, D), BF16),
            vmem((5, 8, SLOTS), F32),
            vmem((16, 8, SLOTS), F32),
            vmem((7, 4, 2, 2, 4, 8, 128), F32),
            vmem((CHUNKS, 4, 2, 4, 8, WIDE), BF16),
            vmem((CHUNKS, 4, 2, 4, 8, WIDE), BF16),
            vmem((CHUNKS, 4, 8, 8, WIDE), BF16),
            vmem((CHUNKS, 3, 8, 8, WIDE), BF16),
            vmem((4, 2, 8, SPLIT), BF16),
            vmem((4, 2, 8, D - SPLIT), BF16),
            vmem((3, 2, 8, SPLIT), BF16),
            vmem((3, 2, 8, D - SPLIT), BF16),
            vmem((2, 8, D), BF16),
            vmem((3, 8, D), BF16),
            vmem((4, 8, D), BF16),
            vmem((4, 2, 2, 4, 8, D), BF16),
            pltpu.SemaphoreType.DMA((TILES + 3,)),
            pltpu.SemaphoreType.DMA((2,)),
            pltpu.SemaphoreType.DMA((N_SEM,)),
            pltpu.SemaphoreType.DMA((N_SEM,)),
        ],
        compiler_params=pltpu.CompilerParams(
            collective_id=0, has_side_effects=True, vmem_limit_bytes=56 << 20
        ),
        name="route",
    )(tokens, slot_keys, norm_gain, w_in, w_out)
    mixed = jnp.dot(combine, gathered.reshape(SLOTS, D), preferred_element_type=F32)
    return mixed.astype(BF16)


def solution(mesh):
    return jax.shard_map(
        on_device,
        mesh=mesh,
        in_specs=(
            P(("seq", "grp"), None),
            P(),
            P(("seq", "grp"), None),
            P(("seq", "grp"), None, None),
            P(("seq", "grp"), None, None),
        ),
        out_specs=P(("seq", "grp"), None),
        check_vma=False,
    )
```

time: 424 us -> 61.7 us (0.15)
  waiting for transfers between devices: 336 us -> 0 us
  Pallas kernels: 0 us -> 54.4 us
  local copies, waits for them, and re-layouts: 27.3 us -> 0 us
  matrix products: 30.5 us -> 7.19 us
  between operations: 13.5 us -> 0.01 us
  starting transfers between devices: 12.1 us -> 0 us
    all_gather x1 -> x0, waiting for transfers between devices: 299 us -> none  [on_device(): gathered = lax.all_gather(expert_out, ('seq', 'grp'), axis=0, tiled=True)]
    pallas_call x0 -> x1, Pallas kernels: none -> 54.4 us  [on_device(): pl.pallas_call(kernel, out_shape=(jax.ShapeDtypeStruct((4, 2, 2, 4, 8, D)...]
    all_to_all x1 -> x0, waiting for transfers between devices: 37.5 us -> none  [in_one_piece(): lax.all_to_all(both, axis, split_axis=split_dim, concat_axis=concat_dim,...]
    dot_general x4 -> x1, matrix products: 30.5 us -> 7.19 us  [on_device(): jnp.dot(combine, gathered.reshape(SLOTS, D), preferred_element_type=F32)]
    all_to_all x1 -> x0, starting transfers between devices: 11.9 us -> none  [in_one_piece(): lax.all_to_all(both, axis, split_axis=split_dim, concat_axis=concat_dim,...]
    concatenate x4 -> x0, local copies, waits for them, and re-layouts: 10.2 us -> none  [in_one_piece(): both = jnp.concatenate(columns, axis=along)]
    slice x2 -> x0, local copies, waits for them, and re-layouts: 4.77 us -> none  [in_one_piece(): piece = out[..., at:at + column.shape[along]]]
    all_to_all x1 -> x0, local copies, waits for them, and re-layouts: 4.4 us -> none  [in_one_piece(): lax.all_to_all(both, axis, split_axis=split_dim, concat_axis=concat_dim,...]
  transfers between devices with their start and end apart: 2 -> 0, of which waited for: 2 -> 0; matrix products, arithmetic and copies ran while one was open for 0% -> 0% of each run, Pallas kernels for 0% -> 0%
where the time goes in v1:
time: 61.7 us; the launch traced here: 61.6 us
  Pallas kernels  54.4 us (88%)
  matrix products  7.19 us (12%)
    pallas_call x1, Pallas kernels, on_device(): pl.pallas_call(kernel, out_shape=(jax.ShapeDtypeStruct((4, 2, 2, 4, 8, D)...  54.4 us
    dot_general x1, matrix products, on_device(): jnp.dot(combine, gathered.reshape(SLOTS, D), preferred_element_type=F32)  7.19 us

profile of v1, /device:TPU:1, one launch (start us, length us, event | category | flops | bytes accessed | tf_op | source)
XLA Modules:
  0.0 61.6 jit_solution(14735914455468615044)
XLA Ops:
  0.0 54.4 %route.1 = (bf16[4,2,2,4,8,1280]{5,4,3,2,1,0:T(8,128)(2,1)}, bf16[2048,512]{1,0:T(8,128)(2,1)}) custom-call(bf16[2048,1280]{1,0:T(8,128)(2,1)} %tok_h.1, bf16[1280,512]{1,0:T(8,128)(2,1)} %key_h.1, f32[1,1280]{1,0:T(1,128)} %gain.1, bf16[1,1280,2560]{2,1,0:T(8,128)(2,1)} %win_h.1, bf16[1,2560,1280]{2,1,0:T(8,128)(2,1)} %wout_h.1), custom_call_target="tpu_custom_call" | custom-call | tf_op jit(solution)/shard_map/route/pallas_call | solution.py:334
  54.4 7.2 %convolution_convert_fusion = bf16[2048,1280]{1,0:T(8,128)(2,1)} fusion(bf16[2048,512]{1,0:T(8,128)(2,1)} %get-tuple-element.7, bf16[512,1280]{1,0:T(8,128)(2,1)} %bitcast.3), kind=kOutput, calls=%fused_computation | convolution fusion | flops 2686976000 | bytes 8650752 | tf_op jit(solution)/shard_map/dot_general | solution.py:376

commit v2 on v0

v2 whole, which is shorter than its diff:
```python
import jax
import jax.numpy as jnp
from jax import lax
from jax.experimental import pallas as pl
from jax.experimental.pallas import tpu as pltpu
from jax.sharding import PartitionSpec as P

F32 = jnp.float32
BF16 = jnp.bfloat16
MESH = pl.DeviceIdType.MESH
TOK, D, FF, SLOTS = 2048, 1280, 2560, 512
LOADS = (256, 256, 512, 1024)
TILE = 512
COLS = (512, 768)
AUX = 128
FAR_FIRST = (2, 1, 3, 0)


def place():
    seq = lax.axis_index("seq")
    grp = lax.axis_index("grp")
    return seq // 4, (seq // 2) % 2, seq % 2, grp // 2, grp % 2


def split3(v):
    hi = v.astype(BF16).astype(F32)
    mid = (v - hi).astype(BF16).astype(F32)
    lo = (v - hi - mid).astype(BF16).astype(F32)
    return hi, mid, lo


def kernel(tok_h, key, gain, win_h, wout_h, g_out, comb_out,
           tok, logit, sct, comb, numer_a, numer_b, win, wout, aux, fcol, fb,
           csend_a, csend_b, crecv_a, crecv_b, sa, sb, ra, rb, x8, gs, g, gf,
           load_sem, out_sem, pair_send, pair_recv, sum_send, sum_recv, row_send, row_recv):
    z, yh, c, x, yl = place()
    y = yh * 2 + yl
    partner = ((z * 2 + yh) * 2 + 1 - c, x * 2 + yl)

    tok_in, at = [], 0
    for i, n in enumerate(LOADS):
        rows = pl.ds(at, n)
        tok_in.append(pltpu.make_async_copy(tok_h.at[rows], tok.at[rows], load_sem.at[i]))
        tok_in[-1].start()
        at += n
    win_in = pltpu.make_async_copy(win_h.at[0], win, load_sem.at[4])
    wout_in = pltpu.make_async_copy(wout_h.at[0], wout, load_sem.at[5])

    def chip(dz, j):
        tz, ty, tx = (z + dz) % 4, (y + j // 4) % 4, (x + j % 4) % 4
        return tz, ty // 2, tx, ty % 2

    def core_of(tz, tyh, tx, tyl):
        return (tz * 2 + tyh) * 2 + c, tx * 2 + tyl

    def every_chip(act):
        for dz in FAR_FIRST:
            def step(j, carry, dz=dz):
                act(dz, j)
                return carry
            lax.fori_loop(0 if dz else 1, 16, step, 0)

    barrier = pltpu.get_barrier_semaphore()
    pl.semaphore_signal(barrier, inc=1, device_id=partner, device_id_type=MESH)

    def greet(dz, j):
        pl.semaphore_signal(barrier, inc=1, device_id=core_of(*chip(dz, j)), device_id_type=MESH)

    every_chip(greet)

    def pair(src, dst, i):
        return pltpu.make_async_remote_copy(
            src_ref=src, dst_ref=dst, send_sem=pair_send.at[i], recv_sem=pair_recv.at[i],
            device_id=partner, device_id_type=MESH)

    peak8 = jnp.full((8, SLOTS), -jnp.inf, F32)
    at = 0
    for i, n in enumerate(LOADS):
        rows = pl.ds(at, n)
        tok_in[i].wait()
        part = jnp.dot(tok[rows], key[...], preferred_element_type=F32)
        logit[rows] = part
        peak8 = jnp.maximum(peak8, jnp.max(part.reshape(n // 8, 8, SLOTS), axis=0))
        at += n
    win_in.start()
    wout_in.start()
    peak = jnp.max(peak8, axis=0, keepdims=True)

    def score_step(t, total8):
        rows = pl.ds(pl.multiple_of(t * TILE, TILE), TILE)
        scores = jnp.exp(logit[rows] - peak)
        sct[:, rows] = scores.astype(BF16).T
        return total8 + jnp.sum(scores.reshape(TILE // 8, 8, SLOTS), axis=0)

    total8 = lax.fori_loop(0, TOK // TILE, score_step, jnp.zeros((8, SLOTS), F32))
    total = jnp.sum(total8, axis=0, keepdims=True)
    row = lax.broadcasted_iota(jnp.int32, (8, SLOTS), 0)
    aux[0] = jnp.where(row == 0, peak, jnp.where(row == 1, total, 0.0))
    pl.semaphore_wait(barrier, 64)
    copies = [pair(aux.at[0], aux.at[1], 0)]
    copies[0].start()

    def numer_part(cols, numer, csend, crecv, i):
        part = jnp.dot(sct[...], tok[:, cols], preferred_element_type=F32)
        numer[...] = part.reshape(numer.shape)
        csend[...] = numer[:, :, 1 - c].astype(BF16)
        copies.append(pair(csend, crecv, i))
        copies[i].start()

    numer_part(pl.ds(0, COLS[0]), numer_a, csend_a, crecv_a, 1)

    copies[0].wait_recv()
    tops, tots = (peak, aux[1][0:1]), (total, aux[1][1:2])
    top = jnp.maximum(*tops)
    factors = [jnp.exp(p - top) for p in tops]
    tot = factors[0] * tots[0] + factors[1] * tots[1]
    line = lax.broadcasted_iota(jnp.int32, (AUX, SLOTS), 0)
    block = jnp.zeros((AUX, SLOTS), F32)
    for i, v in enumerate(split3(top) + split3(tot) + tuple(factors)):
        block = jnp.where(line == i, v, block)
    fcol[...] = block.T.reshape(4, 2, 2, 4, 8, AUX)

    numer_part(pl.ds(COLS[0], COLS[1]), numer_b, csend_b, crecv_b, 2)

    def sum_copy(src, dst, i, target):
        return pltpu.make_async_remote_copy(
            src_ref=src, dst_ref=dst, send_sem=sum_send.at[i], recv_sem=sum_recv.at[i],
            device_id=target, device_id_type=MESH)

    def pair_sum(numer, crecv, s, r, i, n):
        copies[i].wait_recv()

        def step(tz, carry):
            f = fcol[tz, :, c]
            both = numer[tz, :, c] * f[..., 6:7] + crecv[tz].astype(F32) * f[..., 7:8]
            for h in range(2):
                s[tz, :, :, h, :, 0:n] = both[:, :, 4 * h : 4 * h + 4].astype(BF16)
                if i == 1:
                    s[tz, :, :, h, :, n : n + AUX] = f[:, :, 4 * h : 4 * h + 4].astype(BF16)
            return carry

        lax.fori_loop(0, 4, step, 0)

        def give(dz, j):
            to = chip(dz, j)
            sum_copy(s.at[to], r.at[dz * 16 + j], i - 1, core_of(*to)).start()

        every_chip(give)
        pltpu.make_async_copy(s.at[z, yh, x, yl], r.at[0], sum_recv.at[i - 1]).start()

    pair_sum(numer_a, crecv_a, sa, ra, 1, COLS[0])
    pair_sum(numer_b, crecv_b, sb, rb, 2, COLS[1])

    def combine_step(t, carry):
        rows = pl.ds(pl.multiple_of(t * 256, 256), 256)
        e = logit[rows]
        e = jnp.exp(e - jnp.max(e, axis=1, keepdims=True))
        comb[rows] = (e / jnp.sum(e, axis=1, keepdims=True)).astype(BF16)
        return carry

    lax.fori_loop(0, TOK // 256, combine_step, 0)
    comb_copy = pltpu.make_async_copy(comb, comb_out, out_sem.at[0])
    comb_copy.start()

    sum_copy(ra, ra, 0, partner).wait_recv()
    a = ra[:, :, COLS[0] : COLS[0] + AUX].astype(F32)
    tops = a[..., 0:1] + a[..., 1:2] + a[..., 2:3]
    tots = a[..., 3:4] + a[..., 4:5] + a[..., 5:6]
    factor = jnp.exp(tops - jnp.max(tops, axis=0, keepdims=True))
    own_total = jnp.sum(factor * tots, axis=0)
    fb[...] = jnp.broadcast_to(factor, fb.shape)
    own_total = jnp.broadcast_to(own_total, (4, 128))

    def gather_sum(r, k, to):
        cols = pl.ds(k * 128, 128)
        x8[0:4, to : to + 128] = jnp.sum(r[:, :, cols].astype(F32) * fb[...], axis=0) / own_total

    x8[4:8] = jnp.zeros((4, D), F32)
    for k in range(COLS[0] // 128):
        gather_sum(ra, k, k * 128)
    sum_copy(rb, rb, 1, partner).wait_recv()
    for k in range(COLS[1] // 128):
        gather_sum(rb, k, COLS[0] + k * 128)

    normed = (x8[...] * gain[...]).astype(BF16)
    win_in.wait()
    wout_in.wait()
    hidden = jax.nn.gelu(jnp.dot(normed, win[...], preferred_element_type=F32)).astype(BF16)
    gs[...] = jnp.dot(hidden, wout[...], preferred_element_type=F32)[0:4].astype(BF16)

    def row_copy(src, dst, i, target):
        return pltpu.make_async_remote_copy(
            src_ref=src, dst_ref=dst, send_sem=row_send.at[i], recv_sem=row_recv.at[i],
            device_id=target, device_id_type=MESH)

    def show(dz, j):
        row_copy(gs, g.at[z, yh, c, x, yl], dz, core_of(*chip(dz, j))).start()

    every_chip(show)
    pltpu.make_async_copy(gs, g.at[z, yh, c, x, yl], row_recv.at[0]).start()
    for dz in FAR_FIRST:
        slab = g.at[(z + 4 - dz) % 4, :, c]
        row_copy(slab, slab, dz, partner).wait_recv()
        copies.append(pair(slab, slab, 3 + dz))
        copies[-1].start()
    g_copies = []
    for i, dz in enumerate(FAR_FIRST):
        tz = (z + 4 - dz) % 4
        copies[3 + i].wait_recv()
        gf[tz] = g[tz].reshape(128, D)
        g_copies.append(pltpu.make_async_copy(gf.at[tz], g_out.at[tz], out_sem.at[1 + i]))
        g_copies[-1].start()

    for copy in copies:
        copy.wait_send()
    sum_copy(ra.at[pl.ds(0, 63)], ra.at[pl.ds(0, 63)], 0, partner).wait_send()
    sum_copy(rb.at[pl.ds(0, 63)], rb.at[pl.ds(0, 63)], 1, partner).wait_send()
    slab = g.at[0, :, 0]
    for dz in (1, 2, 3):
        row_copy(slab, slab, dz, partner).wait_send()
    part = ra.at[pl.ds(0, 30)]
    row_copy(part, part, 0, partner).wait_send()
    comb_copy.wait()
    for copy in g_copies:
        copy.wait()


def mix_kernel(comb, rows, out):
    out[...] = jnp.dot(comb[...], rows[...], preferred_element_type=F32).astype(BF16)


def on_device(tokens, slot_keys, norm_gain, w_in, w_out):
    anywhere = pl.BlockSpec(memory_space=pl.ANY)
    held = pl.BlockSpec(memory_space=pltpu.VMEM)
    vmem = pltpu.VMEM
    sem = pltpu.SemaphoreType.DMA
    gathered, combine = pl.pallas_call(
        kernel,
        out_shape=(
            jax.ShapeDtypeStruct((4, 128, D), BF16),
            jax.ShapeDtypeStruct((TOK, SLOTS), BF16),
        ),
        in_specs=[anywhere, held, held, anywhere, anywhere],
        out_specs=(anywhere, anywhere),
        scratch_shapes=[
            vmem((TOK, D), BF16),
            vmem((TOK, SLOTS), F32),
            vmem((SLOTS, TOK), BF16),
            vmem((TOK, SLOTS), BF16),
            vmem((4, 2, 2, 4, 8, COLS[0]), F32),
            vmem((4, 2, 2, 4, 8, COLS[1]), F32),
            vmem((D, FF), BF16),
            vmem((FF, D), BF16),
            vmem((2, 8, SLOTS), F32),
            vmem((4, 2, 2, 4, 8, AUX), F32),
            vmem((64, 4, 128), F32),
            vmem((4, 2, 4, 8, COLS[0]), BF16),
            vmem((4, 2, 4, 8, COLS[1]), BF16),
            vmem((4, 2, 4, 8, COLS[0]), BF16),
            vmem((4, 2, 4, 8, COLS[1]), BF16),
            vmem((4, 2, 4, 2, 4, COLS[0] + AUX), BF16),
            vmem((4, 2, 4, 2, 4, COLS[1]), BF16),
            vmem((64, 4, COLS[0] + AUX), BF16),
            vmem((64, 4, COLS[1]), BF16),
            vmem((8, D), F32),
            vmem((4, D), BF16),
            vmem((4, 2, 2, 4, 2, 4, D), BF16),
            vmem((4, 128, D), BF16),
            sem((6,)),
            sem((5,)),
            sem((7,)),
            sem((7,)),
            sem((2,)),
            sem((2,)),
            sem((4,)),
            sem((4,)),
        ],
        compiler_params=pltpu.CompilerParams(
            collective_id=0, has_side_effects=True, vmem_limit_bytes=48 << 20
        ),
        name="route",
    )(tokens, slot_keys, norm_gain, w_in, w_out)
    rows = 256
    return pl.pallas_call(
        mix_kernel,
        out_shape=jax.ShapeDtypeStruct((TOK, D), BF16),
        grid=(TOK // rows,),
        in_specs=[
            pl.BlockSpec((rows, SLOTS), lambda i: (i, 0)),
            pl.BlockSpec((SLOTS, D), lambda i: (0, 0)),
        ],
        out_specs=pl.BlockSpec((rows, D), lambda i: (i, 0)),
        compiler_params=pltpu.CompilerParams(vmem_limit_bytes=12 << 20),
        name="mix",
    )(combine, gathered.reshape(SLOTS, D))


def solution(mesh):
    return jax.shard_map(
        on_device,
        mesh=mesh,
        in_specs=(
            P(("seq", "grp"), None),
            P(),
            P(("seq", "grp"), None),
            P(("seq", "grp"), None, None),
            P(("seq", "grp"), None, None),
        ),
        out_specs=P(("seq", "grp"), None),
        check_vma=False,
    )
```

time: 424 us -> 50.1 us (0.12)
  waiting for transfers between devices: 336 us -> 0 us
  Pallas kernels: 0 us -> 47.9 us
  matrix products: 30.5 us -> 0 us
  local copies, waits for them, and re-layouts: 27.3 us -> 2 us
  between operations: 13.5 us -> 0.01 us
  starting transfers between devices: 12.1 us -> 0 us
    all_gather x1 -> x0, waiting for transfers between devices: 299 us -> none  [on_device(): gathered = lax.all_gather(expert_out, ('seq', 'grp'), axis=0, tiled=True)]
    pallas_call x0 -> x2, Pallas kernels: none -> 47.9 us  [the longest x1 42 us: on_device(): pl.pallas_call(kernel, out_shape=(jax.ShapeDtypeStruct((4, 128, D), BF16)...]
    all_to_all x1 -> x0, waiting for transfers between devices: 37.5 us -> none  [in_one_piece(): lax.all_to_all(both, axis, split_axis=split_dim, concat_axis=concat_dim,...]
    dot_general x4 -> x0, matrix products: 30.5 us -> none  [the longest x1 8.36 us: on_device(): lax.dot_general(weights, tokens, dims, preferred_element_type=jnp.float32)]
    all_to_all x1 -> x0, starting transfers between devices: 11.9 us -> none  [in_one_piece(): lax.all_to_all(both, axis, split_axis=split_dim, concat_axis=concat_dim,...]
    concatenate x4 -> x0, local copies, waits for them, and re-layouts: 10.2 us -> none  [in_one_piece(): both = jnp.concatenate(columns, axis=along)]
    slice x2 -> x0, local copies, waits for them, and re-layouts: 4.77 us -> none  [in_one_piece(): piece = out[..., at:at + column.shape[along]]]
    all_to_all x1 -> x0, local copies, waits for them, and re-layouts: 4.4 us -> none  [in_one_piece(): lax.all_to_all(both, axis, split_axis=split_dim, concat_axis=concat_dim,...]
  transfers between devices with their start and end apart: 2 -> 0, of which waited for: 2 -> 0; matrix products, arithmetic and copies ran while one was open for 0% -> 0% of each run, Pallas kernels for 0% -> 0%
where the time goes in v2:
time: 50.1 us; the launch traced here: 49.9 us
  Pallas kernels  47.9 us (96%)
  local copies, waits for them, and re-layouts  2 us (4%)
    pallas_call x1, Pallas kernels, on_device(): pl.pallas_call(kernel, out_shape=(jax.ShapeDtypeStruct((4, 128, D), BF16)...  42 us
    pallas_call x1, Pallas kernels, on_device(): pl.pallas_call(mix_kernel, out_shape=jax.ShapeDtypeStruct((TOK, D), BF16)...  5.92 us
    unnamed x4, local copies, waits for them, and re-layouts  2 us

profile of v2, /device:TPU:1, one launch (start us, length us, event | category | flops | bytes accessed | tf_op | source)
XLA Modules:
  0.0 49.9 jit_solution(154602216185045911)
XLA Ops:
  0.0 0.0 copy-start
  0.0 1.3 %copy-done = bf16[1280,512]{1,0:T(8,128)(2,1)S(1)} copy-done((bf16[1280,512]{1,0:T(8,128)(2,1)S(1)}, bf16[1280,512]{1,0:T(8,128)(2,1)}, u32[]{:S(2)}) %copy-start) | copy-done | bytes 1310744
  1.3 0.0 copy-start.1
  1.3 0.7 %copy-done.1 = f32[1,1280]{1,0:T(1,128)S(1)} copy-done((f32[1,1280]{1,0:T(1,128)S(1)}, f32[1,1280]{1,0:T(1,128)}, u32[]{:S(2)}) %copy-start.1) | copy-done | bytes 5144
  2.0 42.0 %route.1 = (bf16[4,128,1280]{2,1,0:T(8,128)(2,1)S(1)}, bf16[2048,512]{1,0:T(8,128)(2,1)S(1)}) custom-call(bf16[2048,1280]{1,0:T(8,128)(2,1)} %tok_h.1, bf16[1280,512]{1,0:T(8,128)(2,1)S(1)} %copy-done, f32[1,1280]{1,0:T(1,128)S(1)} %copy-done.1, bf16[1,1280,2560]{2,1,0:T(8,128)(2,1)} %win_h.1, bf16[1,2560,1280]{2,1,0:T(8,128)(2,1)} %wout_h.1), custom_call_target="tpu_custom_call" | custom-call | tf_op jit(solution)/shard_map/route/pallas_call | solution.py:237
  44.0 5.9 %mix.1 = bf16[2048,1280]{1,0:T(8,128)(2,1)} custom-call(bf16[2048,512]{1,0:T(8,128)(2,1)S(1)} %get-tuple-element.7.comb, bf16[512,1280]{1,0:T(8,128)(2,1)S(1)} %bitcast.1), custom_call_target="tpu_custom_call" | custom-call | tf_op jit(solution)/shard_map/mix/pallas_call | solution.py:284
Async XLA Ops:
  0.0 1.3 %copy-start = (bf16[1280,512]{1,0:T(8,128)(2,1)S(1)}, bf16[1280,512]{1,0:T(8,128)(2,1)}, u32[]{:S(2)}) copy-start(bf16[1280,512]{1,0:T(8,128)(2,1)} %key.1) | copy-start | bytes 3932164
  1.3 0.7 %copy-start.1 = (f32[1,1280]{1,0:T(1,128)S(1)}, f32[1,1280]{1,0:T(1,128)}, u32[]{:S(2)}) copy-start(f32[1,1280]{1,0:T(1,128)} %gain.1) | copy-start | bytes 15364

commit v3 on v2

--- a/solution.py
+++ b/solution.py
@@ -11,7 +11,8 @@
 TOK, D, FF, SLOTS = 2048, 1280, 2560, 512
 LOADS = (256, 256, 512, 1024)
 TILE = 512
-COLS = (512, 768)
+COLS = (256, 512, 512)
+START = (0, 256, 768)
 AUX = 128
 FAR_FIRST = (2, 1, 3, 0)
 
@@ -29,10 +30,10 @@
     return hi, mid, lo
 
 
-def kernel(tok_h, key, gain, win_h, wout_h, g_out, comb_out,
-           tok, logit, sct, comb, numer_a, numer_b, win, wout, aux, fcol, fb,
-           csend_a, csend_b, crecv_a, crecv_b, sa, sb, ra, rb, x8, gs, g, gf,
-           load_sem, out_sem, pair_send, pair_recv, sum_send, sum_recv, row_send, row_recv):
+def kernel(tok_h, key, gain_h, win_h, wout_h, g_out, comb_out,
+           tok, logit, sct, comb, numer_a, numer_b, numer_c, gain, win, wout, aux, fcol, fb,
+           csend_a, csend_b, csend_c, crecv_a, crecv_b, crecv_c, sa, sb, sc, ra, rb, rc, x8, gs, g, gf,
+           in_sem, load_sem, out_sem, pair_send, pair_recv, sum_send, sum_recv, row_send, row_recv):
     z, yh, c, x, yl = place()
     y = yh * 2 + yl
     partner = ((z * 2 + yh) * 2 + 1 - c, x * 2 + yl)
@@ -43,6 +44,7 @@
         tok_in.append(pltpu.make_async_copy(tok_h.at[rows], tok.at[rows], load_sem.at[i]))
         tok_in[-1].start()
         at += n
+    gain_in = pltpu.make_async_copy(gain_h, gain, load_sem.at[6])
     win_in = pltpu.make_async_copy(win_h.at[0], win, load_sem.at[4])
     wout_in = pltpu.make_async_copy(wout_h.at[0], wout, load_sem.at[5])
 
@@ -63,10 +65,20 @@
     barrier = pltpu.get_barrier_semaphore()
     pl.semaphore_signal(barrier, inc=1, device_id=partner, device_id_type=MESH)
 
-    def greet(dz, j):
-        pl.semaphore_signal(barrier, inc=1, device_id=core_of(*chip(dz, j)), device_id_type=MESH)
-
-    every_chip(greet)
+    def line(axis, d):
+        if axis == "x":
+            return core_of(z, yh, (x + d) % 4, yl)
+        if axis == "y":
+            ty = (y + d) % 4
+            return core_of(z, ty // 2, x, ty % 2)
+        return core_of((z + d) % 4, yh, x, yl)
+
+    def greet(sem, axes):
+        for axis in axes:
+            for d in (1, 2, 3):
+                pl.semaphore_signal(sem, inc=1, device_id=line(axis, d), device_id_type=MESH)
+
+    greet(barrier, "xyz")
 
     def pair(src, dst, i):
         return pltpu.make_async_remote_copy(
@@ -82,8 +94,15 @@
         logit[rows] = part
         peak8 = jnp.maximum(peak8, jnp.max(part.reshape(n // 8, 8, SLOTS), axis=0))
         at += n
+        if i == 1:
+            pl.semaphore_wait(barrier, 10)
+            greet(in_sem.at[0], "y")
+        if i == 2:
+            pl.semaphore_wait(in_sem.at[0], 3)
+            greet(in_sem.at[1], "z")
     win_in.start()
     wout_in.start()
+    gain_in.start()
     peak = jnp.max(peak8, axis=0, keepdims=True)
 
     def score_step(t, total8):
@@ -96,7 +115,6 @@
     total = jnp.sum(total8, axis=0, keepdims=True)
     row = lax.broadcasted_iota(jnp.int32, (8, SLOTS), 0)
     aux[0] = jnp.where(row == 0, peak, jnp.where(row == 1, total, 0.0))
-    pl.semaphore_wait(barrier, 64)
     copies = [pair(aux.at[0], aux.at[1], 0)]
     copies[0].start()
 
@@ -107,7 +125,9 @@
         copies.append(pair(csend, crecv, i))
         copies[i].start()
 
-    numer_part(pl.ds(0, COLS[0]), numer_a, csend_a, crecv_a, 1)
+    parts = ((numer_a, csend_a, crecv_a, sa, ra), (numer_b, csend_b, crecv_b, sb, rb), (numer_c, csend_c, crecv_c, sc, rc))
+    for i in range(2):
+        numer_part(pl.ds(START[i], COLS[i]), *parts[i][:3], i + 1)
 
     copies[0].wait_recv()
     tops, tots = (peak, aux[1][0:1]), (total, aux[1][1:2])
@@ -120,8 +140,6 @@
         block = jnp.where(line == i, v, block)
     fcol[...] = block.T.reshape(4, 2, 2, 4, 8, AUX)
 
-    numer_part(pl.ds(COLS[0], COLS[1]), numer_b, csend_b, crecv_b, 2)
-
     def sum_copy(src, dst, i, target):
         return pltpu.make_async_remote_copy(
             src_ref=src, dst_ref=dst, send_sem=sum_send.at[i], recv_sem=sum_recv.at[i],
@@ -148,8 +166,11 @@
         every_chip(give)
         pltpu.make_async_copy(s.at[z, yh, x, yl], r.at[0], sum_recv.at[i - 1]).start()
 
-    pair_sum(numer_a, crecv_a, sa, ra, 1, COLS[0])
-    pair_sum(numer_b, crecv_b, sb, rb, 2, COLS[1])
+    pl.semaphore_wait(in_sem.at[1], 3)
+    pair_sum(numer_a, *parts[0][2:], 1, COLS[0])
+    numer_part(pl.ds(START[2], COLS[2]), *parts[2][:3], 3)
+    pair_sum(numer_b, *parts[1][2:], 2, COLS[1])
+    pair_sum(numer_c, *parts[2][2:], 3, COLS[2])
 
     def combine_step(t, carry):
         rows = pl.ds(pl.multiple_of(t * 256, 256), 256)
@@ -176,12 +197,13 @@
         x8[0:4, to : to + 128] = jnp.sum(r[:, :, cols].astype(F32) * fb[...], axis=0) / own_total
 
     x8[4:8] = jnp.zeros((4, D), F32)
-    for k in range(COLS[0] // 128):
-        gather_sum(ra, k, k * 128)
-    sum_copy(rb, rb, 1, partner).wait_recv()
-    for k in range(COLS[1] // 128):
-        gather_sum(rb, k, COLS[0] + k * 128)
-
+    for i, r in enumerate((ra, rb, rc)):
+        if i:
+            sum_copy(r, r, i, partner).wait_recv()
+        for k in range(COLS[i] // 128):
+            gather_sum(r, k, START[i] + k * 128)
+
+    gain_in.wait()
     normed = (x8[...] * gain[...]).astype(BF16)
     win_in.wait()
     wout_in.wait()
@@ -201,32 +223,40 @@
     for dz in FAR_FIRST:
         slab = g.at[(z + 4 - dz) % 4, :, c]
         row_copy(slab, slab, dz, partner).wait_recv()
-        copies.append(pair(slab, slab, 3 + dz))
+        copies.append(pair(slab, slab, 4 + dz))
         copies[-1].start()
     g_copies = []
     for i, dz in enumerate(FAR_FIRST):
         tz = (z + 4 - dz) % 4
-        copies[3 + i].wait_recv()
+        copies[4 + i].wait_recv()
         gf[tz] = g[tz].reshape(128, D)
         g_copies.append(pltpu.make_async_copy(gf.at[tz], g_out.at[tz], out_sem.at[1 + i]))
         g_copies[-1].start()
 
     for copy in copies:
         copy.wait_send()
-    sum_copy(ra.at[pl.ds(0, 63)], ra.at[pl.ds(0, 63)], 0, partner).wait_send()
-    sum_copy(rb.at[pl.ds(0, 63)], rb.at[pl.ds(0, 63)], 1, partner).wait_send()
+    for i, r in enumerate((ra, rb, rc)):
+        sent = r.at[pl.ds(0, 63)]
+        sum_copy(sent, sent, i, partner).wait_send()
     slab = g.at[0, :, 0]
     for dz in (1, 2, 3):
         row_copy(slab, slab, dz, partner).wait_send()
-    part = ra.at[pl.ds(0, 30)]
+    part = ra.at[pl.ds(0, 50)]
     row_copy(part, part, 0, partner).wait_send()
     comb_copy.wait()
     for copy in g_copies:
         copy.wait()
 
 
-def mix_kernel(comb, rows, out):
-    out[...] = jnp.dot(comb[...], rows[...], preferred_element_type=F32).astype(BF16)
+def mix_kernel(comb, rows, out, held, sem):
+    copies = []
+    for k, (at, n) in enumerate(((0, TOK), (0, TOK), (0, TOK), (0, TOK), (0, TOK // 2), (TOK // 2, TOK // 2))):
+        block = (pl.ds(at, n), pl.ds(min(k, 4) * 256, 256))
+        held[block] = jnp.dot(comb[block[0]], rows[:, block[1]], preferred_element_type=F32).astype(BF16)
+        copies.append(pltpu.make_async_copy(held.at[block], out.at[block], sem.at[k]))
+        copies[k].start()
+    for copy in copies:
+        copy.wait()
 
 
 def on_device(tokens, slot_keys, norm_gain, w_in, w_out):
@@ -240,38 +270,35 @@
             jax.ShapeDtypeStruct((4, 128, D), BF16),
             jax.ShapeDtypeStruct((TOK, SLOTS), BF16),
         ),
-        in_specs=[anywhere, held, held, anywhere, anywhere],
+        in_specs=[anywhere, held, anywhere, anywhere, anywhere],
         out_specs=(anywhere, anywhere),
         scratch_shapes=[
             vmem((TOK, D), BF16),
             vmem((TOK, SLOTS), F32),
             vmem((SLOTS, TOK), BF16),
             vmem((TOK, SLOTS), BF16),
-            vmem((4, 2, 2, 4, 8, COLS[0]), F32),
-            vmem((4, 2, 2, 4, 8, COLS[1]), F32),
+            *(vmem((4, 2, 2, 4, 8, n), F32) for n in COLS),
+            vmem((1, D), F32),
             vmem((D, FF), BF16),
             vmem((FF, D), BF16),
             vmem((2, 8, SLOTS), F32),
             vmem((4, 2, 2, 4, 8, AUX), F32),
             vmem((64, 4, 128), F32),
-            vmem((4, 2, 4, 8, COLS[0]), BF16),
-            vmem((4, 2, 4, 8, COLS[1]), BF16),
-            vmem((4, 2, 4, 8, COLS[0]), BF16),
-            vmem((4, 2, 4, 8, COLS[1]), BF16),
-            vmem((4, 2, 4, 2, 4, COLS[0] + AUX), BF16),
-            vmem((4, 2, 4, 2, 4, COLS[1]), BF16),
-            vmem((64, 4, COLS[0] + AUX), BF16),
-            vmem((64, 4, COLS[1]), BF16),
+            *(vmem((4, 2, 4, 8, n), BF16) for n in COLS),
+            *(vmem((4, 2, 4, 8, n), BF16) for n in COLS),
+            *(vmem((4, 2, 4, 2, 4, n), BF16) for n in (COLS[0] + AUX, COLS[1], COLS[2])),
+            *(vmem((64, 4, n), BF16) for n in (COLS[0] + AUX, COLS[1], COLS[2])),
             vmem((8, D), F32),
             vmem((4, D), BF16),
             vmem((4, 2, 2, 4, 2, 4, D), BF16),
             vmem((4, 128, D), BF16),
-            sem((6,)),
+            pltpu.SemaphoreType.REGULAR((2,)),
+            sem((7,)),
             sem((5,)),
-            sem((7,)),
-            sem((7,)),
-            sem((2,)),
-            sem((2,)),
+            sem((8,)),
+            sem((8,)),
+            sem((3,)),
+            sem((3,)),
             sem((4,)),
             sem((4,)),
         ],
@@ -280,16 +307,12 @@
         ),
         name="route",
     )(tokens, slot_keys, norm_gain, w_in, w_out)
-    rows = 256
     return pl.pallas_call(
         mix_kernel,
         out_shape=jax.ShapeDtypeStruct((TOK, D), BF16),
-        grid=(TOK // rows,),
-        in_specs=[
-            pl.BlockSpec((rows, SLOTS), lambda i: (i, 0)),
-            pl.BlockSpec((SLOTS, D), lambda i: (0, 0)),
-        ],
-        out_specs=pl.BlockSpec((rows, D), lambda i: (i, 0)),
+        in_specs=[held, held],
+        out_specs=anywhere,
+        scratch_shapes=[vmem((TOK, D), BF16), sem((6,))],
         compiler_params=pltpu.CompilerParams(vmem_limit_bytes=12 << 20),
         name="mix",
     )(combine, gathered.reshape(SLOTS, D))

time: 50.1 us -> 49.1 us (0.980)
  Pallas kernels: 47.9 us -> 46.9 us
    pallas_call x1, Pallas kernels: 5.92 us -> 4.15 us  [on_device(): pl.pallas_call(mix_kernel, out_shape=jax.ShapeDtypeStruct((TOK, D), BF16)...]
    pallas_call x1, Pallas kernels: 42 us -> 42.8 us  [on_device(): pl.pallas_call(kernel, out_shape=(jax.ShapeDtypeStruct((4, 128, D), BF16)...]
where the time goes in v3:
time: 49.1 us; the launch traced here: 49 us
  Pallas kernels  46.9 us (96%)
  local copies, waits for them, and re-layouts  2 us (4%)
    pallas_call x1, Pallas kernels, on_device(): pl.pallas_call(kernel, out_shape=(jax.ShapeDtypeStruct((4, 128, D), BF16)...  42.8 us
    pallas_call x1, Pallas kernels, on_device(): pl.pallas_call(mix_kernel, out_shape=jax.ShapeDtypeStruct((TOK, D), BF16)...  4.15 us
    unnamed x4, local copies, waits for them, and re-layouts  2 us

profile of v3, /device:TPU:1, one launch (start us, length us, event | category | flops | bytes accessed | tf_op | source)
XLA Modules:
  0.0 49.0 jit_solution(12763829325070013684)
XLA Ops:
  0.0 0.0 copy-start
  0.0 1.3 %copy-done = bf16[1280,512]{1,0:T(8,128)(2,1)S(1)} copy-done((bf16[1280,512]{1,0:T(8,128)(2,1)S(1)}, bf16[1280,512]{1,0:T(8,128)(2,1)}, u32[]{:S(2)}) %copy-start) | copy-done | bytes 1310744
  1.3 0.0 copy-start.1
  1.3 0.7 %copy-done.1 = f32[1,1280]{1,0:T(1,128)S(1)} copy-done((f32[1,1280]{1,0:T(1,128)S(1)}, f32[1,1280]{1,0:T(1,128)}, u32[]{:S(2)}) %copy-start.1) | copy-done | bytes 5144
  2.0 42.8 %route.1 = (bf16[4,128,1280]{2,1,0:T(8,128)(2,1)S(1)}, bf16[2048,512]{1,0:T(8,128)(2,1)S(1)}) custom-call(bf16[2048,1280]{1,0:T(8,128)(2,1)} %tok_h.1, bf16[1280,512]{1,0:T(8,128)(2,1)S(1)} %copy-done, f32[1,1280]{1,0:T(1,128)S(1)} %copy-done.1, bf16[1,1280,2560]{2,1,0:T(8,128)(2,1)} %win_h.1, bf16[1,2560,1280]{2,1,0:T(8,128)(2,1)} %wout_h.1), custom_call_target="tpu_custom_call" | custom-call | tf_op jit(solution)/shard_map/route/pallas_call | solution.py:267
  44.8 4.1 %mix.1 = bf16[2048,1280]{1,0:T(8,128)(2,1)} custom-call(bf16[2048,512]{1,0:T(8,128)(2,1)S(1)} %get-tuple-element.7.comb, bf16[512,1280]{1,0:T(8,128)(2,1)S(1)} %bitcast.1), custom_call_target="tpu_custom_call" | custom-call | tf_op jit(solution)/shard_map/mix/pallas_call | solution.py:310
Async XLA Ops:
  0.0 1.3 %copy-start = (bf16[1280,512]{1,0:T(8,128)(2,1)S(1)}, bf16[1280,512]{1,0:T(8,128)(2,1)}, u32[]{:S(2)}) copy-start(bf16[1280,512]{1,0:T(8,128)(2,1)} %key.1) | copy-start | bytes 3932164
  1.3 0.7 %copy-start.1 = (f32[1,1280]{1,0:T(1,128)S(1)}, f32[1,1280]{1,0:T(1,128)}, u32[]{:S(2)}) copy-start(f32[1,1280]{1,0:T(1,128)} %gain_h.1) | copy-start | bytes 15364

commit v4 on v3

--- a/solution.py
+++ b/solution.py
@@ -14,6 +14,7 @@
 COLS = (256, 512, 512)
 START = (0, 256, 768)
 AUX = 128
+BACK = (768, 512)
 FAR_FIRST = (2, 1, 3, 0)
 
 
@@ -30,14 +31,16 @@
     return hi, mid, lo
 
 
-def kernel(tok_h, key, gain_h, win_h, wout_h, g_out, comb_out,
-           tok, logit, sct, comb, numer_a, numer_b, numer_c, gain, win, wout, aux, fcol, fb,
-           csend_a, csend_b, csend_c, crecv_a, crecv_b, crecv_c, sa, sb, sc, ra, rb, rc, x8, gs, g, gf,
+def kernel(tok_h, key_h, gain_h, win_h, wout_h, g_out, comb_out, mix_out,
+           tok, key, logit, sct, comb, numer_a, numer_b, numer_c, gain, win, wout, aux, fcol, fb,
+           csend_a, csend_b, csend_c, crecv_a, crecv_b, crecv_c, sa, sb, sc, ra, rb, rc, x8, gs_a, gs_b, ga, gb, fa, fb_rows,
            in_sem, load_sem, out_sem, pair_send, pair_recv, sum_send, sum_recv, row_send, row_recv):
     z, yh, c, x, yl = place()
     y = yh * 2 + yl
     partner = ((z * 2 + yh) * 2 + 1 - c, x * 2 + yl)
 
+    key_in = pltpu.make_async_copy(key_h, key, load_sem.at[7])
+    key_in.start()
     tok_in, at = [], 0
     for i, n in enumerate(LOADS):
         rows = pl.ds(at, n)
@@ -85,6 +88,7 @@
             src_ref=src, dst_ref=dst, send_sem=pair_send.at[i], recv_sem=pair_recv.at[i],
             device_id=partner, device_id_type=MESH)
 
+    key_in.wait()
     peak8 = jnp.full((8, SLOTS), -jnp.inf, F32)
     at = 0
     for i, n in enumerate(LOADS):
@@ -208,29 +212,55 @@
     win_in.wait()
     wout_in.wait()
     hidden = jax.nn.gelu(jnp.dot(normed, win[...], preferred_element_type=F32)).astype(BF16)
-    gs[...] = jnp.dot(hidden, wout[...], preferred_element_type=F32)[0:4].astype(BF16)
 
     def row_copy(src, dst, i, target):
         return pltpu.make_async_remote_copy(
             src_ref=src, dst_ref=dst, send_sem=row_send.at[i], recv_sem=row_recv.at[i],
             device_id=target, device_id_type=MESH)
 
-    def show(dz, j):
-        row_copy(gs, g.at[z, yh, c, x, yl], dz, core_of(*chip(dz, j))).start()
-
-    every_chip(show)
-    pltpu.make_async_copy(gs, g.at[z, yh, c, x, yl], row_recv.at[0]).start()
+    def show(gs, g, cols, base):
+        gs[...] = jnp.dot(hidden, wout[:, cols], preferred_element_type=F32)[0:4].astype(BF16)
+
+        def step(dz, j):
+            row_copy(gs, g.at[z, yh, c, x, yl], base + dz, core_of(*chip(dz, j))).start()
+
+        every_chip(step)
+        pltpu.make_async_copy(gs, g.at[z, yh, c, x, yl], row_recv.at[base]).start()
+
+    show(gs_a, ga, pl.ds(0, BACK[0]), 0)
+    show(gs_b, gb, pl.ds(BACK[0], BACK[1]), 4)
+    forwards = {}
+
+    def forward(g, base, dz):
+        slab = g.at[(z + 4 - dz) % 4, :, c]
+        row_copy(slab, slab, base + dz, partner).wait_recv()
+        forwards[base + dz] = pair(slab, slab, 4 + base + dz)
+        forwards[base + dz].start()
+        copies.append(forwards[base + dz])
+
+    def settle(g, f, base, dz):
+        tz = (z + 4 - dz) % 4
+        forwards[base + dz].wait_recv()
+        f[tz] = g[tz].reshape(128, f.shape[2])
+        return tz
+
     for dz in FAR_FIRST:
-        slab = g.at[(z + 4 - dz) % 4, :, c]
-        row_copy(slab, slab, dz, partner).wait_recv()
-        copies.append(pair(slab, slab, 4 + dz))
-        copies[-1].start()
+        forward(ga, 0, dz)
+    for dz in FAR_FIRST:
+        settle(ga, fa, 0, dz)
+    m_copies = []
+    for k in range(BACK[0] // 256):
+        cols = pl.ds(k * 256, 256)
+        tok[:, cols] = jnp.dot(
+            comb[...], fa[:, :, cols].reshape(SLOTS, 256), preferred_element_type=F32).astype(BF16)
+        m_copies.append(pltpu.make_async_copy(tok.at[:, cols], mix_out.at[:, cols], out_sem.at[5 + k]))
+        m_copies[k].start()
+        forward(gb, 4, FAR_FIRST[k])
+    forward(gb, 4, FAR_FIRST[3])
     g_copies = []
     for i, dz in enumerate(FAR_FIRST):
-        tz = (z + 4 - dz) % 4
-        copies[4 + i].wait_recv()
-        gf[tz] = g[tz].reshape(128, D)
-        g_copies.append(pltpu.make_async_copy(gf.at[tz], g_out.at[tz], out_sem.at[1 + i]))
+        tz = settle(gb, fb_rows, 4, dz)
+        g_copies.append(pltpu.make_async_copy(fb_rows.at[tz], g_out.at[tz], out_sem.at[1 + i]))
         g_copies[-1].start()
 
     for copy in copies:
@@ -238,42 +268,51 @@
     for i, r in enumerate((ra, rb, rc)):
         sent = r.at[pl.ds(0, 63)]
         sum_copy(sent, sent, i, partner).wait_send()
-    slab = g.at[0, :, 0]
-    for dz in (1, 2, 3):
-        row_copy(slab, slab, dz, partner).wait_send()
-    part = ra.at[pl.ds(0, 50)]
-    row_copy(part, part, 0, partner).wait_send()
+    for base, g, own in ((0, ga, ra.at[pl.ds(0, 30)]), (4, gb, rb.at[pl.ds(0, 15)])):
+        slab = g.at[0, :, 0]
+        for dz in (1, 2, 3):
+            row_copy(slab, slab, base + dz, partner).wait_send()
+        row_copy(own, own, base, partner).wait_send()
     comb_copy.wait()
-    for copy in g_copies:
+    for copy in g_copies + m_copies:
         copy.wait()
 
 
-def mix_kernel(comb, rows, out, held, sem):
-    copies = []
-    for k, (at, n) in enumerate(((0, TOK), (0, TOK), (0, TOK), (0, TOK), (0, TOK // 2), (TOK // 2, TOK // 2))):
-        block = (pl.ds(at, n), pl.ds(min(k, 4) * 256, 256))
-        held[block] = jnp.dot(comb[block[0]], rows[:, block[1]], preferred_element_type=F32).astype(BF16)
-        copies.append(pltpu.make_async_copy(held.at[block], out.at[block], sem.at[k]))
-        copies[k].start()
+def mix_kernel(comb, rows, first, out, held, sem):
+    copies = [pltpu.make_async_copy(first, out.at[:, pl.ds(0, BACK[0])], sem.at[0])]
+    copies[0].start()
+    half = TOK // 2
+    for k, (at, n, col) in enumerate(((0, TOK, 0), (0, half, 256), (half, half, 256))):
+        here = (pl.ds(at, n), pl.ds(col, 256))
+        held[here] = jnp.dot(comb[pl.ds(at, n)], rows[:, col : col + 256], preferred_element_type=F32).astype(BF16)
+        there = out.at[pl.ds(at, n), pl.ds(BACK[0] + col, 256)]
+        copies.append(pltpu.make_async_copy(held.at[here], there, sem.at[1 + k]))
+        copies[-1].start()
     for copy in copies:
         copy.wait()
 
 
 def on_device(tokens, slot_keys, norm_gain, w_in, w_out):
     anywhere = pl.BlockSpec(memory_space=pl.ANY)
+
+    def stay(v):
+        return pltpu.with_memory_space_constraint(v, pltpu.HBM)
+
     held = pl.BlockSpec(memory_space=pltpu.VMEM)
     vmem = pltpu.VMEM
     sem = pltpu.SemaphoreType.DMA
-    gathered, combine = pl.pallas_call(
+    gathered, combine, first = pl.pallas_call(
         kernel,
         out_shape=(
-            jax.ShapeDtypeStruct((4, 128, D), BF16),
+            jax.ShapeDtypeStruct((4, 128, BACK[1]), BF16),
             jax.ShapeDtypeStruct((TOK, SLOTS), BF16),
+            jax.ShapeDtypeStruct((TOK, BACK[0]), BF16),
         ),
-        in_specs=[anywhere, held, anywhere, anywhere, anywhere],
-        out_specs=(anywhere, anywhere),
+        in_specs=[anywhere] * 5,
+        out_specs=(anywhere,) * 3,
         scratch_shapes=[
             vmem((TOK, D), BF16),
+            vmem((D, SLOTS), BF16),
             vmem((TOK, SLOTS), F32),
             vmem((SLOTS, TOK), BF16),
             vmem((TOK, SLOTS), BF16),
@@ -289,33 +328,33 @@
             *(vmem((4, 2, 4, 2, 4, n), BF16) for n in (COLS[0] + AUX, COLS[1], COLS[2])),
             *(vmem((64, 4, n), BF16) for n in (COLS[0] + AUX, COLS[1], COLS[2])),
             vmem((8, D), F32),
-            vmem((4, D), BF16),
-            vmem((4, 2, 2, 4, 2, 4, D), BF16),
-            vmem((4, 128, D), BF16),
+            *(vmem((4, n), BF16) for n in BACK),
+            *(vmem((4, 2, 2, 4, 2, 4, n), BF16) for n in BACK),
+            *(vmem((4, 128, n), BF16) for n in BACK),
             pltpu.SemaphoreType.REGULAR((2,)),
-            sem((7,)),
-            sem((5,)),
             sem((8,)),
             sem((8,)),
+            sem((12,)),
+            sem((12,)),
             sem((3,)),
             sem((3,)),
-            sem((4,)),
-            sem((4,)),
+            sem((8,)),
+            sem((8,)),
         ],
         compiler_params=pltpu.CompilerParams(
             collective_id=0, has_side_effects=True, vmem_limit_bytes=48 << 20
         ),
         name="route",
-    )(tokens, slot_keys, norm_gain, w_in, w_out)
+    )(*(stay(v) for v in (tokens, slot_keys, norm_gain, w_in, w_out)))
     return pl.pallas_call(
         mix_kernel,
         out_shape=jax.ShapeDtypeStruct((TOK, D), BF16),
-        in_specs=[held, held],
+        in_specs=[held, held, anywhere],
         out_specs=anywhere,
-        scratch_shapes=[vmem((TOK, D), BF16), sem((6,))],
+        scratch_shapes=[vmem((TOK, BACK[1]), BF16), sem((4,))],
         compiler_params=pltpu.CompilerParams(vmem_limit_bytes=12 << 20),
         name="mix",
-    )(combine, gathered.reshape(SLOTS, D))
+    )(combine, gathered.reshape(SLOTS, BACK[1]), first)
 
 
 def solution(mesh):

time: 49.1 us -> 49.5 us (level)
  Pallas kernels: 46.9 us -> 49.4 us
  local copies, waits for them, and re-layouts: 2 us -> 0 us
    pallas_call x1, Pallas kernels: 42.8 us -> 46.2 us  [on_device(): pl.pallas_call(kernel, out_shape=(jax.ShapeDtypeStruct((4, 128, BACK[1]),...]
    unnamed x4 -> x0, local copies, waits for them, and re-layouts: 2 us -> none
    pallas_call x1, Pallas kernels: 4.15 us -> 3.15 us  [on_device(): pl.pallas_call(mix_kernel, out_shape=jax.ShapeDtypeStruct((TOK, D), BF16)...]
where the time goes in v4:
time: 49.5 us; the launch traced here: 49.4 us
  Pallas kernels  49.4 us (100%)
    pallas_call x1, Pallas kernels, on_device(): pl.pallas_call(kernel, out_shape=(jax.ShapeDtypeStruct((4, 128, BACK[1]),...  46.2 us
    pallas_call x1, Pallas kernels, on_device(): pl.pallas_call(mix_kernel, out_shape=jax.ShapeDtypeStruct((TOK, D), BF16)...  3.15 us

profile of v4, /device:TPU:1, one launch (start us, length us, event | category | flops | bytes accessed | tf_op | source)
XLA Modules:
  0.0 49.4 jit_solution(17522390953459263026)
XLA Ops:
  0.0 46.2 %route.1 = (bf16[4,128,512]{2,1,0:T(8,128)(2,1)S(1)}, bf16[2048,512]{1,0:T(8,128)(2,1)S(1)}, bf16[2048,768]{1,0:T(8,128)(2,1)S(1)}) custom-call(bf16[2048,1280]{1,0:T(8,128)(2,1)} %tok_h.1, bf16[1280,512]{1,0:T(8,128)(2,1)} %key_h.1, f32[1,1280]{1,0:T(1,128)} %gain_h.1, bf16[1,1280,2560]{2,1,0:T(8,128)(2,1)} %win_h.1, bf16[1,2560,1280]{2,1,0:T(8,128)(2,1)} %wout_h.1), custom_call_target="tpu_custom_call" | custom-call | tf_op jit(solution)/shard_map/route/pallas_call | solution.py:304
  46.2 3.2 %mix.1 = bf16[2048,1280]{1,0:T(8,128)(2,1)} custom-call(bf16[2048,512]{1,0:T(8,128)(2,1)S(1)} %get-tuple-element.8.comb, bf16[512,512]{1,0:T(8,128)(2,1)S(1)} %bitcast.1, bf16[2048,768]{1,0:T(8,128)(2,1)S(1)} %get-tuple-element.10.first), custom_call_target="tpu_custom_call" | custom-call | tf_op jit(solution)/shard_map/mix/pallas_call | solution.py:349

commit v5 on v3

--- a/solution.py
+++ b/solution.py
@@ -11,8 +11,8 @@
 TOK, D, FF, SLOTS = 2048, 1280, 2560, 512
 LOADS = (256, 256, 512, 1024)
 TILE = 512
-COLS = (256, 512, 512)
-START = (0, 256, 768)
+COLS = (512, 768)
+START = (0, 512)
 AUX = 128
 FAR_FIRST = (2, 1, 3, 0)
 
@@ -30,14 +30,16 @@
     return hi, mid, lo
 
 
-def kernel(tok_h, key, gain_h, win_h, wout_h, g_out, comb_out,
-           tok, logit, sct, comb, numer_a, numer_b, numer_c, gain, win, wout, aux, fcol, fb,
-           csend_a, csend_b, csend_c, crecv_a, crecv_b, crecv_c, sa, sb, sc, ra, rb, rc, x8, gs, g, gf,
-           in_sem, load_sem, out_sem, pair_send, pair_recv, sum_send, sum_recv, row_send, row_recv):
+def kernel(tok_h, key_h, gain_h, win_h, wout_h, g_out, comb_out,
+           tok, key, logit, sct, comb, numer_a, numer_b, gain, win, wout, aux, fcol, fb,
+           csend_a, csend_b, crecv_a, crecv_b, sa, sb, ra, rb, x8, gs, g, gf,
+           in_sem, load_sem, out_sem, pair_out, pair_in, sum_send, sum_recv, row_send, row_recv):
     z, yh, c, x, yl = place()
     y = yh * 2 + yl
     partner = ((z * 2 + yh) * 2 + 1 - c, x * 2 + yl)
 
+    key_in = pltpu.make_async_copy(key_h, key, load_sem.at[7])
+    key_in.start()
     tok_in, at = [], 0
     for i, n in enumerate(LOADS):
         rows = pl.ds(at, n)
@@ -55,8 +57,8 @@
     def core_of(tz, tyh, tx, tyl):
         return (tz * 2 + tyh) * 2 + c, tx * 2 + tyl
 
-    def every_chip(act):
-        for dz in FAR_FIRST:
+    def every_chip(act, steps=FAR_FIRST):
+        for dz in steps:
             def step(j, carry, dz=dz):
                 act(dz, j)
                 return carry
@@ -82,9 +84,10 @@
 
     def pair(src, dst, i):
         return pltpu.make_async_remote_copy(
-            src_ref=src, dst_ref=dst, send_sem=pair_send.at[i], recv_sem=pair_recv.at[i],
+            src_ref=src, dst_ref=dst, send_sem=pair_out.at[i], recv_sem=pair_in.at[i],
             device_id=partner, device_id_type=MESH)
 
+    key_in.wait()
     peak8 = jnp.full((8, SLOTS), -jnp.inf, F32)
     at = 0
     for i, n in enumerate(LOADS):
@@ -118,16 +121,17 @@
     copies = [pair(aux.at[0], aux.at[1], 0)]
     copies[0].start()
 
-    def numer_part(cols, numer, csend, crecv, i):
-        part = jnp.dot(sct[...], tok[:, cols], preferred_element_type=F32)
-        numer[...] = part.reshape(numer.shape)
+    def numer_part(at, n, numer, to):
+        part = jnp.dot(sct[...], tok[:, at : at + n], preferred_element_type=F32)
+        numer[..., to : to + n] = part.reshape(4, 2, 2, 4, 8, n)
+
+    def pair_send(numer, csend, crecv, i):
         csend[...] = numer[:, :, 1 - c].astype(BF16)
         copies.append(pair(csend, crecv, i))
         copies[i].start()
 
-    parts = ((numer_a, csend_a, crecv_a, sa, ra), (numer_b, csend_b, crecv_b, sb, rb), (numer_c, csend_c, crecv_c, sc, rc))
-    for i in range(2):
-        numer_part(pl.ds(START[i], COLS[i]), *parts[i][:3], i + 1)
+    numer_part(0, COLS[0], numer_a, 0)
+    pair_send(numer_a, csend_a, crecv_a, 1)
 
     copies[0].wait_recv()
     tops, tots = (peak, aux[1][0:1]), (total, aux[1][1:2])
@@ -145,7 +149,7 @@
             src_ref=src, dst_ref=dst, send_sem=sum_send.at[i], recv_sem=sum_recv.at[i],
             device_id=target, device_id_type=MESH)
 
-    def pair_sum(numer, crecv, s, r, i, n):
+    def pair_sum(numer, crecv, s, i, n):
         copies[i].wait_recv()
 
         def step(tz, carry):
@@ -159,18 +163,26 @@
 
         lax.fori_loop(0, 4, step, 0)
 
-        def give(dz, j):
+    def give(s, r, i, steps):
+        def step(dz, j):
             to = chip(dz, j)
             sum_copy(s.at[to], r.at[dz * 16 + j], i - 1, core_of(*to)).start()
 
-        every_chip(give)
-        pltpu.make_async_copy(s.at[z, yh, x, yl], r.at[0], sum_recv.at[i - 1]).start()
-
+        every_chip(step, steps)
+        if 0 in steps:
+            pltpu.make_async_copy(s.at[z, yh, x, yl], r.at[0], sum_recv.at[i - 1]).start()
+
+    numer_part(512, 256, numer_b, 0)
     pl.semaphore_wait(in_sem.at[1], 3)
-    pair_sum(numer_a, *parts[0][2:], 1, COLS[0])
-    numer_part(pl.ds(START[2], COLS[2]), *parts[2][:3], 3)
-    pair_sum(numer_b, *parts[1][2:], 2, COLS[1])
-    pair_sum(numer_c, *parts[2][2:], 3, COLS[2])
+    pair_sum(numer_a, crecv_a, sa, 1, COLS[0])
+    give(sa, ra, 1, (2,))
+    numer_part(768, 256, numer_b, 256)
+    give(sa, ra, 1, (1,))
+    numer_part(1024, 256, numer_b, 512)
+    pair_send(numer_b, csend_b, crecv_b, 2)
+    give(sa, ra, 1, (3, 0))
+    pair_sum(numer_b, crecv_b, sb, 2, COLS[1])
+    give(sb, rb, 2, FAR_FIRST)
 
     def combine_step(t, carry):
         rows = pl.ds(pl.multiple_of(t * 256, 256), 256)
@@ -197,7 +209,7 @@
         x8[0:4, to : to + 128] = jnp.sum(r[:, :, cols].astype(F32) * fb[...], axis=0) / own_total
 
     x8[4:8] = jnp.zeros((4, D), F32)
-    for i, r in enumerate((ra, rb, rc)):
+    for i, r in enumerate((ra, rb)):
         if i:
             sum_copy(r, r, i, partner).wait_recv()
         for k in range(COLS[i] // 128):
@@ -223,25 +235,25 @@
     for dz in FAR_FIRST:
         slab = g.at[(z + 4 - dz) % 4, :, c]
         row_copy(slab, slab, dz, partner).wait_recv()
-        copies.append(pair(slab, slab, 4 + dz))
+        copies.append(pair(slab, slab, 3 + dz))
         copies[-1].start()
     g_copies = []
     for i, dz in enumerate(FAR_FIRST):
         tz = (z + 4 - dz) % 4
-        copies[4 + i].wait_recv()
+        copies[3 + i].wait_recv()
         gf[tz] = g[tz].reshape(128, D)
         g_copies.append(pltpu.make_async_copy(gf.at[tz], g_out.at[tz], out_sem.at[1 + i]))
         g_copies[-1].start()
 
     for copy in copies:
         copy.wait_send()
-    for i, r in enumerate((ra, rb, rc)):
+    for i, r in enumerate((ra, rb)):
         sent = r.at[pl.ds(0, 63)]
         sum_copy(sent, sent, i, partner).wait_send()
     slab = g.at[0, :, 0]
     for dz in (1, 2, 3):
         row_copy(slab, slab, dz, partner).wait_send()
-    part = ra.at[pl.ds(0, 50)]
+    part = ra.at[pl.ds(0, 30)]
     row_copy(part, part, 0, partner).wait_send()
     comb_copy.wait()
     for copy in g_copies:
@@ -261,6 +273,10 @@
 
 def on_device(tokens, slot_keys, norm_gain, w_in, w_out):
     anywhere = pl.BlockSpec(memory_space=pl.ANY)
+
+    def stay(v):
+        return pltpu.with_memory_space_constraint(v, pltpu.HBM)
+
     held = pl.BlockSpec(memory_space=pltpu.VMEM)
     vmem = pltpu.VMEM
     sem = pltpu.SemaphoreType.DMA
@@ -270,10 +286,11 @@
             jax.ShapeDtypeStruct((4, 128, D), BF16),
             jax.ShapeDtypeStruct((TOK, SLOTS), BF16),
         ),
-        in_specs=[anywhere, held, anywhere, anywhere, anywhere],
+        in_specs=[anywhere] * 5,
         out_specs=(anywhere, anywhere),
         scratch_shapes=[
             vmem((TOK, D), BF16),
+            vmem((D, SLOTS), BF16),
             vmem((TOK, SLOTS), F32),
             vmem((SLOTS, TOK), BF16),
             vmem((TOK, SLOTS), BF16),
@@ -286,19 +303,19 @@
             vmem((64, 4, 128), F32),
             *(vmem((4, 2, 4, 8, n), BF16) for n in COLS),
             *(vmem((4, 2, 4, 8, n), BF16) for n in COLS),
-            *(vmem((4, 2, 4, 2, 4, n), BF16) for n in (COLS[0] + AUX, COLS[1], COLS[2])),
-            *(vmem((64, 4, n), BF16) for n in (COLS[0] + AUX, COLS[1], COLS[2])),
+            *(vmem((4, 2, 4, 2, 4, n), BF16) for n in (COLS[0] + AUX, COLS[1])),
+            *(vmem((64, 4, n), BF16) for n in (COLS[0] + AUX, COLS[1])),
             vmem((8, D), F32),
             vmem((4, D), BF16),
             vmem((4, 2, 2, 4, 2, 4, D), BF16),
             vmem((4, 128, D), BF16),
             pltpu.SemaphoreType.REGULAR((2,)),
+            sem((8,)),
+            sem((5,)),
             sem((7,)),
-            sem((5,)),
-            sem((8,)),
-            sem((8,)),
-            sem((3,)),
-            sem((3,)),
+            sem((7,)),
+            sem((2,)),
+            sem((2,)),
             sem((4,)),
             sem((4,)),
         ],
@@ -306,7 +323,7 @@
             collective_id=0, has_side_effects=True, vmem_limit_bytes=48 << 20
         ),
         name="route",
-    )(tokens, slot_keys, norm_gain, w_in, w_out)
+    )(*(stay(v) for v in (tokens, slot_keys, norm_gain, w_in, w_out)))
     return pl.pallas_call(
         mix_kernel,
         out_shape=jax.ShapeDtypeStruct((TOK, D), BF16),

time: 49.1 us -> 47.4 us (0.965)
  local copies, waits for them, and re-layouts: 2 us -> 0 us
    unnamed x4 -> x0, local copies, waits for them, and re-layouts: 2 us -> none
where the time goes in v5:
time: 47.4 us; the launch traced here: 47.3 us
  Pallas kernels  47.3 us (100%)
    pallas_call x1, Pallas kernels, on_device(): pl.pallas_call(kernel, out_shape=(jax.ShapeDtypeStruct((4, 128, D), BF16)...  43.2 us
    pallas_call x1, Pallas kernels, on_device(): pl.pallas_call(mix_kernel, out_shape=jax.ShapeDtypeStruct((TOK, D), BF16)...  4.15 us

profile of v5, /device:TPU:1, one launch (start us, length us, event | category | flops | bytes accessed | tf_op | source)
XLA Modules:
  0.0 47.3 jit_solution(9409275224473573617)
XLA Ops:
  0.0 43.2 %route.1 = (bf16[4,128,1280]{2,1,0:T(8,128)(2,1)S(1)}, bf16[2048,512]{1,0:T(8,128)(2,1)S(1)}) custom-call(bf16[2048,1280]{1,0:T(8,128)(2,1)} %tok_h.1, bf16[1280,512]{1,0:T(8,128)(2,1)} %key_h.1, f32[1,1280]{1,0:T(1,128)} %gain_h.1, bf16[1,1280,2560]{2,1,0:T(8,128)(2,1)} %win_h.1, bf16[1,2560,1280]{2,1,0:T(8,128)(2,1)} %wout_h.1), custom_call_target="tpu_custom_call" | custom-call | tf_op jit(solution)/shard_map/route/pallas_call | solution.py:283
  43.2 4.1 %mix.1 = bf16[2048,1280]{1,0:T(8,128)(2,1)} custom-call(bf16[2048,512]{1,0:T(8,128)(2,1)S(1)} %get-tuple-element.7.comb, bf16[512,1280]{1,0:T(8,128)(2,1)S(1)} %bitcast.1), custom_call_target="tpu_custom_call" | custom-call | tf_op jit(solution)/shard_map/mix/pallas_call | solution.py:327

commit v6 on v5

--- a/solution.py
+++ b/solution.py
@@ -50,19 +50,26 @@
     win_in = pltpu.make_async_copy(win_h.at[0], win, load_sem.at[4])
     wout_in = pltpu.make_async_copy(wout_h.at[0], wout, load_sem.at[5])
 
-    def chip(dz, j):
-        tz, ty, tx = (z + dz) % 4, (y + j // 4) % 4, (x + j % 4) % 4
-        return tz, ty // 2, tx, ty % 2
+    zs = [lax.rem(z + d, 4) for d in range(4)]
+    xs = [lax.rem(x + d, 4) for d in range(4)]
+    z_part = [tz * 4 + c for tz in zs]
+    x_part = [tx * 2 for tx in xs]
 
     def core_of(tz, tyh, tx, tyl):
         return (tz * 2 + tyh) * 2 + c, tx * 2 + tyl
 
     def every_chip(act, steps=FAR_FIRST):
         for dz in steps:
-            def step(j, carry, dz=dz):
-                act(dz, j)
+            def along(dy, carry, dz=dz, first=0):
+                ty = lax.rem(y + dy, 4)
+                tyh, tyl = lax.div(ty, 2), lax.rem(ty, 2)
+                for dx in range(first, 4):
+                    device = (z_part[dz] + tyh * 2, x_part[dx] + tyl)
+                    act((zs[dz], tyh, xs[dx], tyl), dz * 16 + dy * 4 + dx, device)
                 return carry
-            lax.fori_loop(0 if dz else 1, 16, step, 0)
+            if dz == 0:
+                along(0, 0, first=1)
+            lax.fori_loop(0 if dz else 1, 4, along, 0)
 
     barrier = pltpu.get_barrier_semaphore()
     pl.semaphore_signal(barrier, inc=1, device_id=partner, device_id_type=MESH)
@@ -164,9 +171,8 @@
         lax.fori_loop(0, 4, step, 0)
 
     def give(s, r, i, steps):
-        def step(dz, j):
-            to = chip(dz, j)
-            sum_copy(s.at[to], r.at[dz * 16 + j], i - 1, core_of(*to)).start()
+        def step(to, number, device):
+            sum_copy(s.at[to], r.at[number], i - 1, device).start()
 
         every_chip(step, steps)
         if 0 in steps:
@@ -227,10 +233,11 @@
             src_ref=src, dst_ref=dst, send_sem=row_send.at[i], recv_sem=row_recv.at[i],
             device_id=target, device_id_type=MESH)
 
-    def show(dz, j):
-        row_copy(gs, g.at[z, yh, c, x, yl], dz, core_of(*chip(dz, j))).start()
-
-    every_chip(show)
+    for dz in FAR_FIRST:
+        def show(to, number, device, dz=dz):
+            row_copy(gs, g.at[z, yh, c, x, yl], dz, device).start()
+
+        every_chip(show, (dz,))
     pltpu.make_async_copy(gs, g.at[z, yh, c, x, yl], row_recv.at[0]).start()
     for dz in FAR_FIRST:
         slab = g.at[(z + 4 - dz) % 4, :, c]

time: 47.4 us -> 47 us (level)
  no operation moved by 1% of the time
where the time goes in v6:
time: 47 us; the launch traced here: 46.9 us
  Pallas kernels  46.9 us (100%)
    pallas_call x1, Pallas kernels, on_device(): pl.pallas_call(kernel, out_shape=(jax.ShapeDtypeStruct((4, 128, D), BF16)...  42.7 us
    pallas_call x1, Pallas kernels, on_device(): pl.pallas_call(mix_kernel, out_shape=jax.ShapeDtypeStruct((TOK, D), BF16)...  4.15 us

profile of v6, /device:TPU:1, one launch (start us, length us, event | category | flops | bytes accessed | tf_op | source)
XLA Modules:
  0.0 46.9 jit_solution(12792408276967153645)
XLA Ops:
  0.0 42.7 %route.1 = (bf16[4,128,1280]{2,1,0:T(8,128)(2,1)S(1)}, bf16[2048,512]{1,0:T(8,128)(2,1)S(1)}) custom-call(bf16[2048,1280]{1,0:T(8,128)(2,1)} %tok_h.1, bf16[1280,512]{1,0:T(8,128)(2,1)} %key_h.1, f32[1,1280]{1,0:T(1,128)} %gain_h.1, bf16[1,1280,2560]{2,1,0:T(8,128)(2,1)} %win_h.1, bf16[1,2560,1280]{2,1,0:T(8,128)(2,1)} %wout_h.1), custom_call_target="tpu_custom_call" | custom-call | tf_op jit(solution)/shard_map/route/pallas_call | solution.py:290
  42.7 4.1 %mix.1 = bf16[2048,1280]{1,0:T(8,128)(2,1)} custom-call(bf16[2048,512]{1,0:T(8,128)(2,1)S(1)} %get-tuple-element.7.comb, bf16[512,1280]{1,0:T(8,128)(2,1)S(1)} %bitcast.1), custom_call_target="tpu_custom_call" | custom-call | tf_op jit(solution)/shard_map/mix/pallas_call | solution.py:334

commit v7 on v6

--- a/solution.py
+++ b/solution.py
@@ -30,9 +30,9 @@
     return hi, mid, lo
 
 
-def kernel(tok_h, key_h, gain_h, win_h, wout_h, g_out, comb_out,
+def kernel(tok_h, key_h, gain_h, win_h, wout_h, gf, comb_out,
            tok, key, logit, sct, comb, numer_a, numer_b, gain, win, wout, aux, fcol, fb,
-           csend_a, csend_b, crecv_a, crecv_b, sa, sb, ra, rb, x8, gs, g, gf,
+           csend_a, csend_b, crecv_a, crecv_b, sa, sb, ra, rb, x8, gs, g,
            in_sem, load_sem, out_sem, pair_out, pair_in, sum_send, sum_recv, row_send, row_recv):
     z, yh, c, x, yl = place()
     y = yh * 2 + yl
@@ -244,13 +244,10 @@
         row_copy(slab, slab, dz, partner).wait_recv()
         copies.append(pair(slab, slab, 3 + dz))
         copies[-1].start()
-    g_copies = []
     for i, dz in enumerate(FAR_FIRST):
         tz = (z + 4 - dz) % 4
         copies[3 + i].wait_recv()
         gf[tz] = g[tz].reshape(128, D)
-        g_copies.append(pltpu.make_async_copy(gf.at[tz], g_out.at[tz], out_sem.at[1 + i]))
-        g_copies[-1].start()
 
     for copy in copies:
         copy.wait_send()
@@ -263,8 +260,6 @@
     part = ra.at[pl.ds(0, 30)]
     row_copy(part, part, 0, partner).wait_send()
     comb_copy.wait()
-    for copy in g_copies:
-        copy.wait()
 
 
 def mix_kernel(comb, rows, out, held, sem):
@@ -294,7 +289,7 @@
             jax.ShapeDtypeStruct((TOK, SLOTS), BF16),
         ),
         in_specs=[anywhere] * 5,
-        out_specs=(anywhere, anywhere),
+        out_specs=(held, anywhere),
         scratch_shapes=[
             vmem((TOK, D), BF16),
             vmem((D, SLOTS), BF16),
@@ -315,10 +310,9 @@
             vmem((8, D), F32),
             vmem((4, D), BF16),
             vmem((4, 2, 2, 4, 2, 4, D), BF16),
-            vmem((4, 128, D), BF16),
             pltpu.SemaphoreType.REGULAR((2,)),
             sem((8,)),
-            sem((5,)),
+            sem((1,)),
             sem((7,)),
             sem((7,)),
             sem((2,)),

time: 47 us -> 46.8 us (level)
  no operation moved by 1% of the time
where the time goes in v7:
time: 46.8 us; the launch traced here: 46.7 us
  Pallas kernels  46.7 us (100%)
    pallas_call x1, Pallas kernels, on_device(): pl.pallas_call(kernel, out_shape=(jax.ShapeDtypeStruct((4, 128, D), BF16)...  42.6 us
    pallas_call x1, Pallas kernels, on_device(): pl.pallas_call(mix_kernel, out_shape=jax.ShapeDtypeStruct((TOK, D), BF16)...  4.15 us

profile of v7, /device:TPU:1, one launch (start us, length us, event | category | flops | bytes accessed | tf_op | source)
XLA Modules:
  0.0 46.7 jit_solution(10619269917696666576)
XLA Ops:
  0.0 42.6 %route.1 = (bf16[4,128,1280]{2,1,0:T(8,128)(2,1)S(1)}, bf16[2048,512]{1,0:T(8,128)(2,1)S(1)}) custom-call(bf16[2048,1280]{1,0:T(8,128)(2,1)} %tok_h.1, bf16[1280,512]{1,0:T(8,128)(2,1)} %key_h.1, f32[1,1280]{1,0:T(1,128)} %gain_h.1, bf16[1,1280,2560]{2,1,0:T(8,128)(2,1)} %win_h.1, bf16[1,2560,1280]{2,1,0:T(8,128)(2,1)} %wout_h.1), custom_call_target="tpu_custom_call" | custom-call | tf_op jit(solution)/shard_map/route/pallas_call | solution.py:285
  42.6 4.1 %mix.1 = bf16[2048,1280]{1,0:T(8,128)(2,1)} custom-call(bf16[2048,512]{1,0:T(8,128)(2,1)S(1)} %get-tuple-element.7.comb, bf16[512,1280]{1,0:T(8,128)(2,1)S(1)} %bitcast.1), custom_call_target="tpu_custom_call" | custom-call | tf_op jit(solution)/shard_map/mix/pallas_call | solution.py:328
